TPU v7x, 128 devices: a whole 4x4x4 slice. The times are simulated.
128 devices in a mesh: az: 16 (over x_lo, z, core), el: 8 (over x_hi, y).
Axes of the slice: x: 4 (x_hi: 2, x_lo: 2; x = x_hi * 2 + x_lo), y: 4, z: 4, core: 2. Of those that a mesh axis runs over, the one named last changes fastest.
Arguments:
- points: bfloat16 [16, 4096, 256], P('el', 'az'), may hold values from -6 to 6
- skip: bfloat16 [16, 4096, 256], P('el', 'az'), may hold values from -6 to 6
- tokens: bfloat16 [16, 8, 128, 256], P('az', 'el')
- send_slots: int32 [16, 8, 5, 8, 16], P('az', 'el'), may hold values from 0 to 127
- recv_idx: int32 [16, 4096, 16], P('el', 'az'), may hold values from 0 to 639, as said below
- w_query: bfloat16 [256, 256], replicated, may hold values from -0.375 to 0.375
- w_key: bfloat16 [256, 256], replicated, may hold values from -0.375 to 0.375
- w_value: bfloat16 [256, 256], replicated, may hold values from -0.375 to 0.375
- w_out: bfloat16 [256, 256], replicated, may hold values from -0.375 to 0.375
- w_hid: bfloat16 [256, 1024], replicated, may hold values from -0.375 to 0.375
- w_skip: bfloat16 [256, 1024], replicated, may hold values from -0.375 to 0.375
- w_down: bfloat16 [1024, 256], replicated, may hold values from -0.1875 to 0.1875
- w_conv: bfloat16 [9, 256, 256], replicated, may hold values from -0.125 to 0.125
Outputs:
- refined: bfloat16 [16, 4096, 256], P('el', 'az')
Inputs may be any that keep to these rules, and one draw needn't show every extreme that they name: send_slots[o, e, j, f, k] is the row of owner device (o, e)'s tokens sent as slot k to the device of azimuth block (o + j - 2) mod 16 and elevation block f. `recv_idx`: an entry (j * 8 + e) * 16 + k names slot k of what the device of elevation block e, 2 - j azimuth blocks away, sends to the point's device. For each requesting device and each such owner only the slots below a live count of 1 to 16 are named; each requesting device has its own block's slots from itself all live.
All inputs are finite; a program needn't handle non-finite values.
Results may differ from a plain program's by a relative error of at most 0.01.
Values may be sent and summed in bfloat16 or wider, within the bound.
A program may use at most 64 MiB of HBM per device.

v0:
```python
import math

import jax
import jax.numpy as jnp
from jax import lax
from jax.sharding import PartitionSpec as P

HEADS = 8
REACH = 2


def passed_along(x, axis, by):
    length = lax.axis_size(axis)
    return lax.ppermute(x, axis, [(i, (i + by) % length) for i in range(length)])


def with_halo(cells, sides, width, closed):
    for axis, dim in sides:
        count = lax.axis_size(axis)
        ends = count if closed else count - 1
        head = lax.slice_in_dim(cells, 0, width, axis=dim)
        tail = lax.slice_in_dim(cells, cells.shape[dim] - width, cells.shape[dim], axis=dim)
        cells = jnp.concatenate(
            [
                lax.ppermute(tail, axis, [(i, (i + 1) % count) for i in range(ends)]),
                cells,
                lax.ppermute(head, axis, [((i + 1) % count, i) for i in range(ends)]),
            ],
            axis=dim,
        )
    return cells


def normalize(features):
    widened = features.astype(jnp.float32)
    return widened * lax.rsqrt(jnp.mean(widened * widened, axis=-1, keepdims=True) + 1e-06)


def project_tokens(token_block, w_key, w_value):
    key_rows = jnp.dot(token_block, w_key, preferred_element_type=jnp.float32).astype(jnp.bfloat16)
    normed_tokens = normalize(token_block).astype(jnp.bfloat16)
    value_rows = jnp.dot(normed_tokens, w_value, preferred_element_type=jnp.float32).astype(
        jnp.bfloat16
    )
    return (key_rows, value_rows)


def per_device(
    points,
    skip,
    tokens,
    send_slots,
    recv_idx,
    w_query,
    w_key,
    w_value,
    w_out,
    w_hid,
    w_skip,
    w_down,
    w_conv,
):
    point_rows, point_cols, feature_width = points.shape
    point_count = point_rows * point_cols
    head_width = feature_width // HEADS
    neighbours = recv_idx.shape[2]
    own_tokens = tokens[0, 0]
    slot_table = send_slots[0, 0]
    offset_count, group_count, capacity = slot_table.shape
    own_keys, own_values = project_tokens(own_tokens, w_key, w_value)
    source_table = jnp.concatenate([own_keys, own_values], axis=1)
    row_width = source_table.shape[1]
    payload = jnp.take(source_table, slot_table.reshape(-1), axis=0).reshape(
        offset_count, group_count, capacity, row_width
    )
    swapped = lax.all_to_all(payload, "el", split_axis=1, concat_axis=1, tiled=True)
    arrived = []
    for offset in range(offset_count):
        if offset == REACH:
            arrived.append(swapped[offset])
        else:
            arrived.append(passed_along(swapped[offset], "az", offset - REACH))
    received = jnp.stack(arrived)
    table_rows = offset_count * group_count * capacity
    received = received.reshape(table_rows, row_width)
    key_rows = received[:, :feature_width]
    value_rows = received[:, feature_width:]
    key_heads = key_rows.reshape(table_rows, HEADS, head_width)
    value_heads = value_rows.reshape(table_rows, HEADS, head_width)
    flat_points = points.reshape(point_count, feature_width)
    query = jnp.dot(flat_points, w_query, preferred_element_type=jnp.float32).astype(jnp.bfloat16)
    block_size = min(512, point_count)
    block_count = point_count // block_size
    scale_factor = 1.0 / math.sqrt(head_width)
    slot_iota = jnp.arange(table_rows, dtype=jnp.int32)

    def attend(inputs):
        query_block, index_block = inputs
        one_hot = (index_block[:, :, None] == slot_iota[None, None, :]).astype(jnp.bfloat16)
        full_scores = jnp.einsum(
            "bhd,thd->bht", query_block, key_heads, preferred_element_type=jnp.float32
        )
        high_part = full_scores.astype(jnp.bfloat16)
        rest_part = full_scores - high_part.astype(jnp.float32)
        middle_part = rest_part.astype(jnp.bfloat16)
        low_part = (rest_part - middle_part.astype(jnp.float32)).astype(jnp.bfloat16)
        picked = jnp.einsum("bnt,bht->bhn", one_hot, high_part, preferred_element_type=jnp.float32)
        picked = picked + jnp.einsum(
            "bnt,bht->bhn", one_hot, middle_part, preferred_element_type=jnp.float32
        )
        picked = picked + jnp.einsum(
            "bnt,bht->bhn", one_hot, low_part, preferred_element_type=jnp.float32
        )
        scores = picked * scale_factor
        shifted = jnp.exp(scores - jnp.max(scores, axis=-1, keepdims=True))
        weights = (shifted / jnp.sum(shifted, axis=-1, keepdims=True)).astype(jnp.bfloat16)
        spread = jnp.einsum("bhn,bnt->bht", weights, one_hot, preferred_element_type=jnp.float32)
        spread_high = spread.astype(jnp.bfloat16)
        spread_low = (spread - spread_high.astype(jnp.float32)).astype(jnp.bfloat16)
        combined = jnp.einsum(
            "bht,thd->bhd", spread_high, value_heads, preferred_element_type=jnp.float32
        )
        combined = combined + jnp.einsum(
            "bht,thd->bhd", spread_low, value_heads, preferred_element_type=jnp.float32
        )
        return combined.reshape(block_size, feature_width).astype(jnp.bfloat16)

    attended = lax.map(
        attend,
        (
            query.reshape(block_count, block_size, HEADS, head_width),
            recv_idx.reshape(block_count, block_size, neighbours),
        ),
    )
    attended = attended.reshape(point_count, feature_width)
    residual_sum = flat_points.astype(jnp.float32) + jnp.dot(
        attended, w_out, preferred_element_type=jnp.float32
    )
    normed = normalize(residual_sum).astype(jnp.bfloat16)
    flat_skip = skip.reshape(point_count, feature_width)
    hidden_pre = jnp.dot(normed, w_hid, preferred_element_type=jnp.float32) + jnp.dot(
        flat_skip, w_skip, preferred_element_type=jnp.float32
    )
    inner = jax.nn.gelu(hidden_pre, approximate=True).astype(jnp.bfloat16)
    joined = residual_sum + jnp.dot(inner, w_down, preferred_element_type=jnp.float32)
    conv_input = (
        normalize(joined).astype(jnp.bfloat16).reshape(point_rows, point_cols, feature_width)
    )
    widened = with_halo(conv_input, (("az", 1),), 1, True)
    padded = with_halo(widened, (("el", 0),), 1, False)
    refined = joined
    for tap_index in range(9):
        row_step = tap_index // 3
        col_step = tap_index % 3
        window = padded[row_step : row_step + point_rows, col_step : col_step + point_cols].reshape(
            point_count, feature_width
        )
        refined = refined + jnp.dot(window, w_conv[tap_index], preferred_element_type=jnp.float32)
    return refined.astype(jnp.bfloat16).reshape(point_rows, point_cols, feature_width)


def solution(mesh):
    return jax.shard_map(
        per_device,
        mesh=mesh,
        in_specs=(
            P("el", "az", None),
            P("el", "az", None),
            P("az", "el", None, None),
            P("az", "el", None, None, None),
            P("el", "az", None),
            P(),
            P(),
            P(),
            P(),
            P(),
            P(),
            P(),
            P(),
        ),
        out_specs=P("el", "az", None),
        check_vma=False,
    )
```

profile of v0, /device:TPU:24, one launch (start us, length us, event | category | flops | bytes accessed | tf_op | source)
XLA Modules:
  0.0 139.4 jit_solution(4217562837387891698)
XLA Ops:
  0.0 0.9 reshape_squeeze.6
  0.9 0.7 compare_and_fusion
  1.6 0.9 fusion.40
  2.6 1.1 convolution_convert_fusion.2
  3.7 1.1 convolution_convert_fusion.1
  4.9 2.8 %gather_fusion = bf16[640,512]{1,0:T(8,128)(2,1)S(1)} fusion(bf16[128,512]{1,0:T(8,128)(2,1)S(1)} %pad_maximum_fusion.4, s32[1024]{0:T(1024)S(1)} %pad_clamp_fusion), kind=kCustom, calls=%fused_computation | custom fusion | bytes 1313280 | tf_op jit(solution)/shard_map/jit(_take)/gather | solution.py:73
  7.7 1.0 copy_select_fusion
  8.7 7.1 %all-to-all-start = ((bf16[5,8,16,512]{3,2,0,1:T(8,128)(2,1)}), bf16[5,8,16,512]{3,2,0,1:T(8,128)(2,1)S(1)}, u32[]{:S(2)}, u32[]{:S(2)}) async-start(bf16[5,8,16,512]{3,2,0,1:T(8,128)(2,1)} %copy_select_fusion), calls=%async_computation | async-start | bytes 1310720 | tf_op jit(solution)/shard_map/all_to_all | solution.py:76
  16.0 10.2 %all-to-all-done = bf16[5,8,16,512]{3,2,0,1:T(8,128)(2,1)S(1)} async-done(((bf16[5,8,16,512]{3,2,0,1:T(8,128)(2,1)}), bf16[5,8,16,512]{3,2,0,1:T(8,128)(2,1)S(1)}, u32[]{:S(2)}, u32[]{:S(2)}) %all-to-all-start) | async-done | bytes 655392 | tf_op jit(solution)/shard_map/all_to_all | solution.py:76
  26.3 4.2 %collective-permute-start = (bf16[8,16,512]{2,1,0:T(8,128)(2,1)S(1)}, bf16[8,16,512]{2,1,0:T(8,128)(2,1)S(1)}, u32[]{:S(2)}, u32[]{:S(2)}) collective-permute-start(bf16[8,16,512]{2,1,0:T(8,128)(2,1)S(1)} %get-tuple-element.35), channel_id=1, source_target_pairs={{0,112},{8,120},{16,0},{24,8},{32,16},{40,24},{48,32},{56,40},{64,... | collective-permute-start | bytes 393224 | tf_op jit(solution)/shard_map/ppermute | solution.py:14
  30.4 0.3 convolution_convert_fusion
  30.8 0.5 collective-permute-start.2
  31.3 1.7 %collective-permute-done = bf16[8,16,512]{2,1,0:T(8,128)(2,1)S(1)} collective-permute-done((bf16[8,16,512]{2,1,0:T(8,128)(2,1)S(1)}, bf16[8,16,512]{2,1,0:T(8,128)(2,1)S(1)}, u32[]{:S(2)}, u32[]{:S(2)}) %collective-permute-start) | collective-permute-done | bytes 131104 | tf_op jit(solution)/shard_map/ppermute | solution.py:14
  33.0 1.4 collective-permute-done.1
  34.4 3.4 %collective-permute-done.2 = bf16[8,16,512]{2,1,0:T(8,128)(2,1)S(1)} collective-permute-done((bf16[8,16,512]{2,1,0:T(8,128)(2,1)S(1)}, bf16[8,16,512]{2,1,0:T(8,128)(2,1)S(1)}, u32[]{:S(2)}, u32[]{:S(2)}) %collective-permute-start.2) | collective-permute-done | bytes 131104 | tf_op jit(solution)/shard_map/ppermute | solution.py:14
  37.8 2.0 %collective-permute-done.3 = bf16[8,16,512]{2,1,0:T(8,128)(2,1)S(1)} collective-permute-done((bf16[8,16,512]{2,1,0:T(8,128)(2,1)S(1)}, bf16[8,16,512]{2,1,0:T(8,128)(2,1)S(1)}, u32[]{:S(2)}, u32[]{:S(2)}) %collective-permute-start.3) | collective-permute-done | bytes 131104 | tf_op jit(solution)/shard_map/ppermute | solution.py:14
  39.8 0.2 copy.37
  40.0 6.6 %fusion.9 = (bf16[512,8,640]{0,2,1:T(8,128)(2,1)}, bf16[512,8,640]{0,2,1:T(8,128)(2,1)}, bf16[8,640,512]{2,1,0:T(8,128)(2,1)}) fusion(bf16[640,8,32]{0,2,1:T(8,128)(2,1)S(1)} %bitcast.138, bf16[512,8,32]{0,2,1:T(8,128)(2,1)S(1)} %bitcast.139), kind=kOutput, calls=%fused_computation.15 | convolution fusion | flops 188743680 | bytes 16318464 | tf_op jit(solution)/shard_map/while/body/eval_jaxpr/bhd,thd->bht/dot_general | solution.py:100
  46.7 9.2 %copy.42 = bf16[512,8,640]{2,1,0:T(8,128)(2,1)} copy(bf16[512,8,640]{0,2,1:T(8,128)(2,1)} %get-tuple-element.20) | data formatting | bytes 10485760 | tf_op jit(solution)/shard_map/while/body/eval_jaxpr/convert_element_type | solution.py:106
  55.8 9.2 %copy.41 = bf16[512,8,640]{2,1,0:T(8,128)(2,1)} copy(bf16[512,8,640]{0,2,1:T(8,128)(2,1)} %get-tuple-element.19) | data formatting | bytes 10485760 | tf_op jit(solution)/shard_map/while/body/eval_jaxpr/convert_element_type | solution.py:105
  65.0 7.6 %fusion.2 = f32[512,8,16]{2,1,0:T(8,128)} fusion(bf16[512,8,640]{2,1,0:T(8,128)(2,1)} %copy.42, s32[512,16]{1,0:T(8,128)S(1)} %bitcast.152), kind=kOutput, calls=%fused_computation.4 | convolution fusion | flops 89128960 | bytes 5537792 | tf_op jit(solution)/shard_map/while/body/eval_jaxpr/bnt,bht->bhn/dot_general | solution.py:111
  72.6 5.8 %fusion.3 = f32[512,8,16]{2,1,0:T(8,128)} fusion(bf16[512,8,640]{2,1,0:T(8,128)(2,1)S(1)} %copy-done.1, s32[512,16]{1,0:T(8,128)S(1)} %bitcast.153), kind=kOutput, calls=%fused_computation.5 | convolution fusion | flops 89128960 | bytes 5537792 | tf_op jit(solution)/shard_map/while/body/eval_jaxpr/bnt,bht->bhn/dot_general | solution.py:108
  78.4 9.2 %copy.40 = bf16[512,8,640]{2,1,0:T(8,128)(2,1)} copy(bf16[512,8,640]{0,2,1:T(8,128)(2,1)} %bitcast.130) | data formatting | bytes 10485760 | tf_op jit(solution)/shard_map/while/body/eval_jaxpr/convert_element_type | solution.py:103
  87.6 0.2 copy.36
  87.8 14.0 %fusion.77 = (f32[512,8]{1,0:T(8,128)S(1)}, f32[512,8,16]{2,1,0:T(8,128)}) fusion(f32[512,8,16]{2,1,0:T(8,128)} %fusion.2, f32[512,8,16]{2,1,0:T(8,128)} %fusion.3, bf16[512,8,640]{2,1,0:T(8,128)(2,1)} %copy.40, s32[512,16]{1,0:T(8,128)S(1)} %bitcast.154), kind=kOutput, calls=%fused_computation.122 | convolution fusion | flops 89456656 | bytes 6078464 | tf_op jit(solution)/shard_map/while/body/eval_jaxpr/sub | solution.py:115
  101.8 6.2 %subtract_convert_fusion = (bf16[512,8,640]{2,1,0:T(8,128)(2,1)S(1)}, bf16[512,8,640]{2,1,0:T(8,128)(2,1)S(1)}) fusion(s32[512,16]{1,0:T(8,128)S(1)} %bitcast.155, f32[512,8,16]{2,1,0:T(8,128)} %get-tuple-element.52, f32[512,8]{1,0:T(8,128)S(1)} %get-tuple-element.51), kind=kOutput, calls=%fused_computation.9 | convolution fusion | flops 99745792 | bytes 10797056 | tf_op jit(solution)/shard_map/while/body/eval_jaxpr/bhn,bnt->bht/dot_general | solution.py:117
  108.0 1.7 %fusion.10 = f32[8,32,512]{2,1,0:T(8,128)S(1)} fusion(bf16[640,8,32]{0,2,1:T(8,128)(2,1)S(1)} %bitcast.135, bf16[512,8,640]{2,1,0:T(8,128)(2,1)S(1)} %get-tuple-element.17), kind=kOutput, calls=%fused_computation.16 | convolution fusion | flops 167772160 | bytes 6094848 | tf_op jit(solution)/shard_map/while/body/eval_jaxpr/bht,thd->bhd/dot_general | solution.py:123
  109.7 1.8 %fusion.29 = bf16[8,32,512]{2,1,0:T(8,128)(2,1)S(1)} fusion(f32[8,32,512]{2,1,0:T(8,128)S(1)} %fusion.10, bf16[640,8,32]{0,2,1:T(8,128)(2,1)S(1)} %bitcast.136, bf16[512,8,640]{2,1,0:T(8,128)(2,1)S(1)} %get-tuple-element.18), kind=kOutput, calls=%fused_computation.45 | convolution fusion | flops 168034304 | bytes 6356992 | tf_op jit(solution)/shard_map/while/body/eval_jaxpr/bht,thd->bhd/dot_general | solution.py:120
  111.5 0.4 multiply_reduce_fusion.1
  112.0 0.5 fusion.38
  112.4 0.3 copy-done.2
  112.7 2.5 %multiply_reduce_fusion = (f32[512]{0:T(512)S(1)}, f32[512,256]{1,0:T(8,128)S(1)}) fusion(f32[512,256]{1,0:T(8,128)} %copy-done.2, bf16[1024,256]{1,0:T(8,128)(2,1)} %param.24, f32[512,1024]{1,0:T(8,128)S(1)} %fusion.38, bf16[512,256]{1,0:T(8,128)(2,1)S(1)} %bitcast.156, bf16[256,1024]{1,0:T(8,128)(2,1)} %param.23), kind=kOutput, calls=%fused_computation.57 | convolution fusion | flops 542506496 | bytes 4458496 | tf_op jit(solution)/shard_map/dot_general | solution.py:145
  115.4 0.3 collective-permute-start.4
  115.7 3.6 %collective-permute-start.5 = (bf16[2,1,256]{2,1,0:T(2,128)(2,1)S(1)}, bf16[2,1,256]{2,1,0:T(2,128)(2,1)S(1)}, u32[]{:S(2)}, u32[]{:S(2)}) collective-permute-start(bf16[2,1,256]{2,1,0:T(2,128)(2,1)S(1)} %get-tuple-element.49), channel_id=1, source_target_pairs={{8,0},{16,8},{24,16},{32,24},{40,32},{48,40},{56,48},{64,56},{72,6... | collective-permute-start | bytes 3080 | tf_op jit(solution)/shard_map/ppermute | solution.py:27
  119.3 1.3 collective-permute-done.4
  120.7 5.1 %collective-permute-start.6 = (bf16[1,258,256]{2,1,0:T(8,128)(2,1)S(1)}, bf16[1,258,256]{2,1,0:T(8,128)(2,1)S(1)}, u32[]{:S(2)}, u32[]{:S(2)}) collective-permute-start(bf16[1,258,256]{2,1,0:T(8,128)(2,1)S(1)} %get-tuple-element.42), channel_id=1, source_target_pairs={{0,1},{1,2},{2,3},{3,4},{4,5},{5,6},{6,7},{8,9},{9,10},{10,11},{11... | collective-permute-start | bytes 396296 | tf_op jit(solution)/shard_map/ppermute | solution.py:25
  125.9 1.9 %collective-permute-start.7 = (bf16[1,258,256]{2,1,0:T(8,128)(2,1)S(1)}, bf16[1,258,256]{2,1,0:T(8,128)(2,1)S(1)}, u32[]{:S(2)}, u32[]{:S(2)}) collective-permute-start(bf16[1,258,256]{2,1,0:T(8,128)(2,1)S(1)} %get-tuple-element.43), channel_id=1, source_target_pairs={{1,0},{2,1},{3,2},{4,3},{5,4},{6,5},{7,6},{9,8},{10,9},{11,10},{12... | collective-permute-start | bytes 396296 | tf_op jit(solution)/shard_map/ppermute | solution.py:27
  127.8 1.1 fusion.48
  129.1 7.3 %collective-permute-done.7 = bf16[1,258,256]{2,1,0:T(8,128)(2,1)S(1)} collective-permute-done((bf16[1,258,256]{2,1,0:T(8,128)(2,1)S(1)}, bf16[1,258,256]{2,1,0:T(8,128)(2,1)S(1)}, u32[]{:S(2)}, u32[]{:S(2)}) %collective-permute-start.7) | collective-permute-done | bytes 132128 | tf_op jit(solution)/shard_map/ppermute | solution.py:27
  136.5 0.3 fusion.73
  136.8 0.2 convolution_add_fusion.6
  137.0 0.2 fusion.45
  137.3 0.2 convolution_add_fusion.5
  137.5 0.2 convolution_add_fusion.4
  137.7 0.2 fusion.24
  138.0 0.2 fusion.23
  138.2 0.2 convolution_add_fusion.1
  138.4 0.9 fusion.32
  (42 shorter events, 0.9 us)
Async XLA Ops:
  0.0 112.0 %copy-start = (bf16[256,1024]{1,0:T(8,128)(2,1)S(1)}, bf16[256,1024]{1,0:T(8,128)(2,1)}, u32[]{:S(2)}) copy-start(bf16[256,1024]{1,0:T(8,128)(2,1)} %param.22) | copy-start | bytes 1572868
  7.7 8.2 %copy-start.7 = (s32[2,256,16]{1,2,0:T(8,128)S(1)}, s32[2,256,16]{1,2,0:T(8,128)}, u32[]{:S(2)}) copy-start(s32[2,256,16]{1,2,0:T(8,128)} %param.17) | copy-start | bytes 98308
  7.7 22.7 %copy-start.4 = (bf16[2,256,256]{2,1,0:T(8,128)(2,1)S(1)}, bf16[2,256,256]{2,1,0:T(8,128)(2,1)}, u32[]{:S(2)}) copy-start(bf16[2,256,256]{2,1,0:T(8,128)(2,1)} %param.13) | copy-start | bytes 786436
  7.7 22.7 %copy-start.5 = (bf16[256,256]{1,0:T(8,128)(2,1)S(1)}, bf16[256,256]{1,0:T(8,128)(2,1)}, u32[]{:S(2)}) copy-start(bf16[256,256]{1,0:T(8,128)(2,1)} %param.18) | copy-start | bytes 393220
  8.7 17.5 %all-to-all-start = ((bf16[5,8,16,512]{3,2,0,1:T(8,128)(2,1)}), bf16[5,8,16,512]{3,2,0,1:T(8,128)(2,1)S(1)}, u32[]{:S(2)}, u32[]{:S(2)}) async-start(bf16[5,8,16,512]{3,2,0,1:T(8,128)(2,1)} %copy_select_fusion), calls=%async_computation | async-start | bytes 1310720 | tf_op jit(solution)/shard_map/all_to_all | solution.py:76
  26.3 6.7 %collective-permute-start = (bf16[8,16,512]{2,1,0:T(8,128)(2,1)S(1)}, bf16[8,16,512]{2,1,0:T(8,128)(2,1)S(1)}, u32[]{:S(2)}, u32[]{:S(2)}) collective-permute-start(bf16[8,16,512]{2,1,0:T(8,128)(2,1)S(1)} %get-tuple-element.35), channel_id=1, source_target_pairs={{0,112},{8,120},{16,0},{24,8},{32,16},{40,24},{48,32},{56,40},{64,... | collective-permute-start | bytes 393224 | tf_op jit(solution)/shard_map/ppermute | solution.py:14
  30.7 3.6 %collective-permute-start.1 = (bf16[8,16,512]{2,1,0:T(8,128)(2,1)S(1)}, bf16[8,16,512]{2,1,0:T(8,128)(2,1)S(1)}, u32[]{:S(2)}, u32[]{:S(2)}) collective-permute-start(bf16[8,16,512]{2,1,0:T(8,128)(2,1)S(1)} %get-tuple-element.34), channel_id=1, source_target_pairs={{0,120},{8,0},{16,8},{24,16},{32,24},{40,32},{48,40},{56,48},{64,5... | collective-permute-start | bytes 393224 | tf_op jit(solution)/shard_map/ppermute | solution.py:14
  30.8 7.0 %collective-permute-start.2 = (bf16[8,16,512]{2,1,0:T(8,128)(2,1)S(1)}, bf16[8,16,512]{2,1,0:T(8,128)(2,1)S(1)}, u32[]{:S(2)}, u32[]{:S(2)}) collective-permute-start(bf16[8,16,512]{2,1,0:T(8,128)(2,1)S(1)} %get-tuple-element.33), channel_id=1, source_target_pairs={{0,8},{8,16},{16,24},{24,32},{32,40},{40,48},{48,56},{56,64},{64,7... | collective-permute-start | bytes 393224 | tf_op jit(solution)/shard_map/ppermute | solution.py:14
  31.3 8.5 %collective-permute-start.3 = (bf16[8,16,512]{2,1,0:T(8,128)(2,1)S(1)}, bf16[8,16,512]{2,1,0:T(8,128)(2,1)S(1)}, u32[]{:S(2)}, u32[]{:S(2)}) collective-permute-start(bf16[8,16,512]{2,1,0:T(8,128)(2,1)S(1)} %get-tuple-element.32), channel_id=1, source_target_pairs={{0,16},{8,24},{16,32},{24,40},{32,48},{40,56},{48,64},{56,72},{64,... | collective-permute-start | bytes 393224 | tf_op jit(solution)/shard_map/ppermute | solution.py:14
  65.0 7.6 %copy-start.1 = (bf16[512,8,640]{2,1,0:T(8,128)(2,1)S(1)}, bf16[512,8,640]{2,1,0:T(8,128)(2,1)}, u32[]{:S(2)}) copy-start(bf16[512,8,640]{2,1,0:T(8,128)(2,1)} %copy.41) | copy-start | bytes 15728644
  109.7 1.8 %copy-start.6 = (bf16[256,256]{1,0:T(8,128)(2,1)S(1)}, bf16[256,256]{1,0:T(8,128)(2,1)}, u32[]{:S(2)}) copy-start(bf16[256,256]{1,0:T(8,128)(2,1)} %param.21) | copy-start | bytes 393220
  111.5 1.2 copy-start.8
  111.9 0.8 copy-start.2
  115.4 5.2 %collective-permute-start.4 = (bf16[2,1,256]{2,1,0:T(2,128)(2,1)S(1)}, bf16[2,1,256]{2,1,0:T(2,128)(2,1)S(1)}, u32[]{:S(2)}, u32[]{:S(2)}) collective-permute-start(bf16[2,1,256]{2,1,0:T(2,128)(2,1)S(1)} %get-tuple-element.48), channel_id=1, source_target_pairs={{0,8},{8,16},{16,24},{24,32},{32,40},{40,48},{48,56},{56,64},{64,7... | collective-permute-start | bytes 3080 | tf_op jit(solution)/shard_map/ppermute | solution.py:25
  115.7 4.9 %collective-permute-start.5 = (bf16[2,1,256]{2,1,0:T(2,128)(2,1)S(1)}, bf16[2,1,256]{2,1,0:T(2,128)(2,1)S(1)}, u32[]{:S(2)}, u32[]{:S(2)}) collective-permute-start(bf16[2,1,256]{2,1,0:T(2,128)(2,1)S(1)} %get-tuple-element.49), channel_id=1, source_target_pairs={{8,0},{16,8},{24,16},{32,24},{40,32},{48,40},{56,48},{64,56},{72,6... | collective-permute-start | bytes 3080 | tf_op jit(solution)/shard_map/ppermute | solution.py:27
  120.7 8.3 %collective-permute-start.6 = (bf16[1,258,256]{2,1,0:T(8,128)(2,1)S(1)}, bf16[1,258,256]{2,1,0:T(8,128)(2,1)S(1)}, u32[]{:S(2)}, u32[]{:S(2)}) collective-permute-start(bf16[1,258,256]{2,1,0:T(8,128)(2,1)S(1)} %get-tuple-element.42), channel_id=1, source_target_pairs={{0,1},{1,2},{2,3},{3,4},{4,5},{5,6},{6,7},{8,9},{9,10},{10,11},{11... | collective-permute-start | bytes 396296 | tf_op jit(solution)/shard_map/ppermute | solution.py:25
  125.9 10.5 %collective-permute-start.7 = (bf16[1,258,256]{2,1,0:T(8,128)(2,1)S(1)}, bf16[1,258,256]{2,1,0:T(8,128)(2,1)S(1)}, u32[]{:S(2)}, u32[]{:S(2)}) collective-permute-start(bf16[1,258,256]{2,1,0:T(8,128)(2,1)S(1)} %get-tuple-element.43), channel_id=1, source_target_pairs={{1,0},{2,1},{3,2},{4,3},{5,4},{6,5},{7,6},{9,8},{10,9},{11,10},{12... | collective-permute-start | bytes 396296 | tf_op jit(solution)/shard_map/ppermute | solution.py:27
  129.1 7.7 %copy-start.3 = (bf16[9,256,256]{2,1,0:T(8,128)(2,1)S(1)}, bf16[9,256,256]{2,1,0:T(8,128)(2,1)}, u32[]{:S(2)}) copy-start(bf16[9,256,256]{2,1,0:T(8,128)(2,1)} %param.25) | copy-start | bytes 3538948
where the time goes:
time: 140 us; the launch traced here: 139 us
  matrix products  53.2 us (38%)
  local copies, waits for them, and re-layouts  32.5 us (23%)
  waiting for transfers between devices  27.2 us (19%)
  starting transfers between devices  22.9 us (16%)
  other arithmetic  3.16 us (2%)
    sub x1, matrix products, attend(): shifted = jnp.exp(scores - jnp.max(scores, axis=-1, keepdims=True))  14 us
    all_to_all x1, waiting for transfers between devices, per_device(): lax.all_to_all(payload, 'el', split_axis=1, concat_axis=1, tiled=True)  10.2 us
    convert_element_type x1, local copies, waits for them, and re-layouts, attend(): middle_part = rest_part.astype(jnp.bfloat16)  9.19 us
    convert_element_type x1, local copies, waits for them, and re-layouts, attend(): (rest_part - middle_part.astype(jnp.float32)).astype(jnp.bfloat16)  9.16 us
    convert_element_type x1, local copies, waits for them, and re-layouts, attend(): high_part = full_scores.astype(jnp.bfloat16)  9.15 us
    ppermute x4, waiting for transfers between devices, passed_along(): lax.ppermute(x, axis, [(i, (i + by) % length) for i in range(length)])  8.41 us
    dot_general x1, matrix products, attend(): jnp.einsum('bnt,bht->bhn', one_hot, low_part, preferred_element_type=jnp....  7.56 us
    ppermute x2, waiting for transfers between devices, with_halo(): lax.ppermute(head, axis, [((i + 1) % count, i) for i in range(ends)])  7.36 us
  transfers between devices with their start and end apart: 9, of which 7 were waited for; matrix products, arithmetic and copies ran while one was open for 1% of the time, Pallas kernels for 0%

commit v1 on v0

v1 whole, which is shorter than its diff:
```python
import math

import jax
import jax.numpy as jnp
from jax import lax
from jax.experimental import pallas as pl
from jax.experimental.pallas import tpu as pltpu
from jax.sharding import PartitionSpec as P

D = 256
HEADS = 8
HEAD = D // HEADS
FF = 1024
NEAR = 16
REACH = 2
OFFSETS = 5
CAP = 16
TOK = 128
COLS = 256
EL = 8
AZ = 16
SLOTS = OFFSETS * EL
TABLE = SLOTS * CAP
POINTS = 512
HALF = 256
PAD = 16
FAR = -1e30
MESH = pl.DeviceIdType.MESH
BF16 = jnp.bfloat16
F32 = jnp.float32

SEGMENTS = (
    (0, 0, 0, 64, 0),
    (0, 0, 192, 64, 64),
    (0, 1, 0, 64, 128),
    (0, 1, 192, 64, 192),
    (1, 0, 64, 128, 0),
    (1, 1, 64, 128, 128),
)


def nt(a, b):
    return lax.dot_general(a, b, (((1,), (1,)), ((), ())), preferred_element_type=F32)


def nn(a, b):
    return lax.dot_general(a, b, (((1,), (0,)), ((), ())), preferred_element_type=F32)


def inv_rms(x):
    return lax.rsqrt(jnp.mean(x * x, axis=-1, keepdims=True) + 1e-06)


def gelu(u):
    inner = math.sqrt(2.0 / math.pi) * (u + 0.044715 * (u * u * u))
    return 0.5 * u * (1.0 + jnp.tanh(inner))


def kernel(
    points_hbm,
    skip_hbm,
    tokens_hbm,
    slots_hbm,
    index_hbm,
    wq_hbm,
    wk_hbm,
    wv_hbm,
    wo_hbm,
    wh_hbm,
    ws_hbm,
    wd_hbm,
    wc_hbm,
    out_ref,
    pts,
    skp,
    tok,
    slt,
    idx,
    wq,
    wk,
    wv,
    wo,
    wh,
    ws,
    wd,
    wc,
    payload,
    recv,
    qmt,
    hs,
    bias,
    kbuf,
    vt,
    att,
    joined,
    cin,
    wvt,
    in_sem,
    send_sem,
    recv_sem,
    halo_send,
    halo_recv,
):
    az = lax.axis_index("az")
    el = lax.axis_index("el")

    def az_at(step):
        return lax.rem(az + step + AZ, AZ)

    def el_at(step):
        return lax.rem(el + step, EL)

    def load(number, src, dst):
        copy = pltpu.make_async_copy(src, dst, in_sem.at[number])
        copy.start()
        return copy

    tok_in = load(0, tokens_hbm.at[0, 0], tok)
    slt_in = load(1, slots_hbm.at[0, 0], slt)
    wq_in = load(2, wq_hbm, wq)
    pts_in = []
    idx_in = []
    skp_in = []
    for number, (chunk, row, col, width, place) in enumerate(SEGMENTS):
        here = pl.ds(chunk * HALF + place, width)
        pts_in.append(load(3 + number, points_hbm.at[row, pl.ds(col, width)], pts.at[here]))
        idx_in.append(load(9 + number, index_hbm.at[row, pl.ds(col, width)], idx.at[here]))
    for number, (chunk, row, col, width, place) in enumerate(SEGMENTS):
        here = pl.ds(chunk * HALF + place, width)
        skp_in.append(load(15 + number, skip_hbm.at[row, pl.ds(col, width)], skp.at[here]))
    ws_in = load(21, ws_hbm, ws)
    wk_in = load(22, wk_hbm, wk)
    wv_in = load(23, wv_hbm, wv)
    wo_in = load(24, wo_hbm, wo)
    wh_in = load(25, wh_hbm, wh)
    wd_in = load(26, wd_hbm, wd)
    wc_in = load(27, wc_hbm, wc)

    barrier = pltpu.get_barrier_semaphore()

    def greet(number, carry):
        j = lax.div(number, EL)
        r = lax.rem(number, EL)

        @pl.when(number != REACH * EL)
        def _():
            pl.semaphore_signal(
                barrier,
                inc=1,
                device_id={"az": az_at(j - REACH), "el": el_at(r)},
                device_id_type=MESH,
            )

        return carry

    lax.fori_loop(0, SLOTS, greet, 0)

    slt_in.wait()
    tok_in.wait()
    eye = (
        lax.broadcasted_iota(jnp.int32, (NEAR, NEAR), 0)
        == lax.broadcasted_iota(jnp.int32, (NEAR, NEAR), 1)
    ).astype(F32).astype(BF16)
    slot_cols = nt(eye, slt[...].reshape(SLOTS, CAP).astype(F32).astype(BF16))
    lane_id = lax.broadcasted_iota(jnp.int32, (CAP, TOK), 1).astype(F32)
    picks = jnp.concatenate(
        [
            (jnp.broadcast_to(slot_cols[:, s : s + 1], (CAP, TOK)) == lane_id)
            .astype(F32)
            .astype(BF16)
            for s in range(SLOTS)
        ],
        axis=0,
    )
    payload[...] = nn(picks, tok[...]).astype(BF16).reshape(SLOTS, CAP, D)

    wq_in.wait()
    for copy in pts_in:
        copy.wait()
    query_t = (nt(wq[...].T, pts[...]) * (1.0 / math.sqrt(HEAD) / math.log(2.0))).astype(BF16)
    zero_rows = jnp.zeros((HEAD, POINTS), BF16)
    for h in range(HEADS):
        for part in range(4):
            rows = pl.ds(part * HEAD, HEAD)
            if part == h % 4:
                qmt[h, rows, :] = query_t[h * HEAD : (h + 1) * HEAD, :]
            else:
                qmt[h, rows, :] = zero_rows

    pl.semaphore_wait(barrier, SLOTS - 1)

    def token_copy(j, r):
        f = el_at(r)
        return pltpu.make_async_remote_copy(
            src_ref=payload.at[j * EL + f],
            dst_ref=recv.at[j * EL + el],
            send_sem=send_sem.at[j * EL + f],
            recv_sem=recv_sem.at[j * EL + el],
            device_id={"az": az_at(j - REACH), "el": f},
            device_id_type=MESH,
        )

    for r in (4, 6, 2, 5, 7, 3, 1, 0):
        for j in range(OFFSETS):
            if (j, r) != (REACH, 0):
                token_copy(j, r).start()
    recv[REACH * EL + el] = payload[REACH * EL + el]

    for copy in idx_in:
        copy.wait()
    entries = idx[...]
    low = nt(eye, (entries & (TOK - 1)).astype(F32).astype(BF16)).astype(jnp.int32)
    high = nt(eye, lax.shift_right_logical(entries, 7).astype(F32).astype(BF16)).astype(jnp.int32)
    unit = lax.shift_left(jnp.ones_like(high), high * 5)

    down = lax.broadcasted_iota(jnp.int32, (8, POINTS), 0)
    for block in range(TOK // 8):
        total = jnp.zeros((8, POINTS), jnp.int32)
        for n in range(NEAR):
            hit = jnp.broadcast_to(low[n : n + 1, :] - block * 8, (8, POINTS)) == down
            total = total + jnp.where(hit, jnp.broadcast_to(unit[n : n + 1, :], (8, POINTS)), 0)
        for group in range(OFFSETS):
            count = lax.shift_right_logical(total, 5 * group) & 31
            logs = jnp.log(count.astype(F32)) * (1.0 / math.log(2.0))
            bias[pl.ds(group * TOK + block * 8, 8), :] = jnp.where(count > 0, logs, FAR)

    for copy in skp_in:
        copy.wait()
    ws_in.wait()
    for block in range(FF // D):
        cols = pl.ds(block * D, D)
        hs[:, cols] = nn(skp[...], ws[:, cols])

    wv_in.wait()
    wvt[...] = wv[...].T
    vt[:, pl.ds(HEAD, 16), :] = jnp.ones((HEADS, 16, TABLE), BF16)

    @pl.when(el == 0)
    def _():
        cin[0, :, :] = jnp.zeros((COLS + 2 * PAD, D), BF16)

    @pl.when(el == EL - 1)
    def _():
        cin[3, :, :] = jnp.zeros((COLS + 2 * PAD, D), BF16)

    wk_in.wait()
    for j in range(OFFSETS):
        for r in range(EL):
            if (j, r) != (REACH, 0):
                e = el_at(r)
                pltpu.make_async_remote_copy(
                    src_ref=payload.at[j * EL + e],
                    dst_ref=recv.at[j * EL + e],
                    send_sem=send_sem.at[j * EL + e],
                    recv_sem=recv_sem.at[j * EL + e],
                    device_id={"az": az_at(REACH - j), "el": e},
                    device_id_type=MESH,
                ).wait_recv()
    rows = recv[...].reshape(TABLE, D)
    kbuf[...] = nn(rows, wk[...]).astype(BF16)
    wide = rows.astype(F32)
    normed_tokens = (wide * inv_rms(wide)).astype(BF16)
    value_t = nt(wvt[...], normed_tokens).astype(BF16)
    for h in range(HEADS):
        vt[h, pl.ds(0, HEAD), :] = value_t[h * HEAD : (h + 1) * HEAD, :]

    wo_in.wait()
    wh_in.wait()
    wd_in.wait()

    def halo(number, src, dst, device):
        return pltpu.make_async_remote_copy(
            src_ref=src,
            dst_ref=dst,
            send_sem=halo_send.at[number],
            recv_sem=halo_recv.at[number],
            device_id=device,
            device_id_type=MESH,
        )

    here = {"az": az, "el": el}
    west, east = az_at(-1), az_at(1)
    above = jnp.maximum(el - 1, 0)
    below = jnp.minimum(el + 1, EL - 1)
    first, last = pl.ds(PAD, PAD), pl.ds(COLS, PAD)
    left_pad, right_pad = pl.ds(0, PAD), pl.ds(PAD + COLS, PAD)

    def up_copies(chunk):
        if chunk == 1:
            mid = pl.ds(PAD + 64, 128)
            return [halo(0, cin.at[1, mid], cin.at[3, mid], {"az": az, "el": above})]
        one, two = pl.ds(PAD, 64), pl.ds(PAD + 192, 64)
        return [
            halo(1, cin.at[1, one], cin.at[3, one], {"az": az, "el": above}),
            halo(2, cin.at[1, two], cin.at[3, two], {"az": az, "el": above}),
            halo(3, cin.at[1, first], cin.at[3, right_pad], {"az": west, "el": above}),
            halo(4, cin.at[1, last], cin.at[3, left_pad], {"az": east, "el": above}),
        ]

    def down_copies(chunk):
        if chunk == 1:
            mid = pl.ds(PAD + 64, 128)
            return [halo(5, cin.at[2, mid], cin.at[0, mid], {"az": az, "el": below})]
        one, two = pl.ds(PAD, 64), pl.ds(PAD + 192, 64)
        return [
            halo(6, cin.at[2, one], cin.at[0, one], {"az": az, "el": below}),
            halo(7, cin.at[2, two], cin.at[0, two], {"az": az, "el": below}),
            halo(8, cin.at[2, first], cin.at[0, right_pad], {"az": west, "el": below}),
            halo(9, cin.at[2, last], cin.at[0, left_pad], {"az": east, "el": below}),
        ]

    def side_copies():
        return [
            halo(10, cin.at[1, first], cin.at[1, right_pad], {"az": west, "el": el}),
            halo(11, cin.at[2, first], cin.at[2, right_pad], {"az": west, "el": el}),
            halo(12, cin.at[1, last], cin.at[1, left_pad], {"az": east, "el": el}),
            halo(13, cin.at[2, last], cin.at[2, left_pad], {"az": east, "el": el}),
        ]

    for chunk in range(2):
        span = pl.ds(chunk * HALF, HALF)
        for h in range(HEADS):
            lanes = pl.ds((h // 4) * 128, 128)
            scores = nn(kbuf[:, lanes], qmt[h, :, span]) + bias[:, span]
            top = jnp.max(scores, axis=0, keepdims=True)
            weights = jnp.exp2((scores - top).astype(BF16))
            summed = nn(vt[h], weights)
            share = summed[:HEAD, :] * (1.0 / summed[HEAD : HEAD + 1, :])
            att[pl.ds(h * HEAD, HEAD), :] = share
        attended = att[...].T.astype(BF16)
        residual = pts[span, :].astype(F32) + nn(attended, wo[...])
        normed = (residual * inv_rms(residual)).astype(BF16)
        total = residual
        for block in range(FF // D):
            cols = pl.ds(block * D, D)
            hidden = gelu(nn(normed, wh[:, cols]) + hs[span, cols]).astype(BF16)
            total = total + nn(hidden, wd[cols, :])
        conv_in = (total * inv_rms(total)).astype(BF16)
        for c, row, col, width, place in SEGMENTS:
            if c == chunk:
                joined[row, pl.ds(col, width), :] = total[place : place + width, :]
                cin[1 + row, pl.ds(PAD + col, width), :] = conv_in[place : place + width, :]

        @pl.when(el > 0)
        def _():
            for copy in up_copies(chunk):
                copy.start()

        @pl.when(el < EL - 1)
        def _():
            for copy in down_copies(chunk):
                copy.start()

        if chunk == 0:
            for copy in side_copies():
                copy.start()

    for copy in side_copies():
        copy.wait_recv()
    wc_in.wait()

    def taps(row):
        return [cin[row, pl.ds(PAD + step, COLS), :] for step in (-1, 0, 1)]

    own = jnp.concatenate(taps(1) + taps(2), axis=1)
    upper = joined[0] + nn(own, wc[pl.ds(3, 6)].reshape(6 * D, D))
    lower = joined[1] + nn(own, wc[pl.ds(0, 6)].reshape(6 * D, D))

    @pl.when(el > 0)
    def _():
        for chunk in range(2):
            for copy in down_copies(chunk):
                copy.wait_recv()

    @pl.when(el < EL - 1)
    def _():
        for chunk in range(2):
            for copy in up_copies(chunk):
                copy.wait_recv()

    upper = upper + nn(jnp.concatenate(taps(0), axis=1), wc[pl.ds(0, 3)].reshape(3 * D, D))
    lower = lower + nn(jnp.concatenate(taps(3), axis=1), wc[pl.ds(6, 3)].reshape(3 * D, D))
    out_ref[0] = upper.astype(BF16)
    out_ref[1] = lower.astype(BF16)

    for j in range(OFFSETS):
        for r in range(EL):
            if (j, r) != (REACH, 0):
                token_copy(j, r).wait_send()
    for copy in side_copies():
        copy.wait_send()

    @pl.when(el > 0)
    def _():
        for chunk in range(2):
            for copy in up_copies(chunk):
                copy.wait_send()

    @pl.when(el < EL - 1)
    def _():
        for chunk in range(2):
            for copy in down_copies(chunk):
                copy.wait_send()


def per_device(*args):
    any_spec = pl.BlockSpec(memory_space=pl.ANY)
    return pl.pallas_call(
        kernel,
        out_shape=jax.ShapeDtypeStruct((2, COLS, D), BF16),
        in_specs=[any_spec] * len(args),
        out_specs=pl.BlockSpec(memory_space=pltpu.VMEM),
        scratch_shapes=[
            pltpu.VMEM((POINTS, D), BF16),
            pltpu.VMEM((POINTS, D), BF16),
            pltpu.VMEM((TOK, D), BF16),
            pltpu.VMEM((OFFSETS, EL, CAP), jnp.int32),
            pltpu.VMEM((POINTS, NEAR), jnp.int32),
            pltpu.VMEM((D, D), BF16),
            pltpu.VMEM((D, D), BF16),
            pltpu.VMEM((D, D), BF16),
            pltpu.VMEM((D, D), BF16),
            pltpu.VMEM((D, FF), BF16),
            pltpu.VMEM((D, FF), BF16),
            pltpu.VMEM((FF, D), BF16),
            pltpu.VMEM((9, D, D), BF16),
            pltpu.VMEM((SLOTS, CAP, D), BF16),
            pltpu.VMEM((SLOTS, CAP, D), BF16),
            pltpu.VMEM((HEADS, D // 2, POINTS), BF16),
            pltpu.VMEM((POINTS, FF), F32),
            pltpu.VMEM((TABLE, POINTS), F32),
            pltpu.VMEM((TABLE, D), BF16),
            pltpu.VMEM((HEADS, HEAD + 16, TABLE), BF16),
            pltpu.VMEM((D, HALF), F32),
            pltpu.VMEM((2, COLS, D), F32),
            pltpu.VMEM((4, COLS + 2 * PAD, D), BF16),
            pltpu.VMEM((D, D), BF16),
            pltpu.SemaphoreType.DMA((28,)),
            pltpu.SemaphoreType.DMA((SLOTS,)),
            pltpu.SemaphoreType.DMA((SLOTS,)),
            pltpu.SemaphoreType.DMA((14,)),
            pltpu.SemaphoreType.DMA((14,)),
        ],
        compiler_params=pltpu.CompilerParams(
            collective_id=0, has_side_effects=True, vmem_limit_bytes=56 * 1024 * 1024
        ),
        name="decoder",
    )(*args)


def solution(mesh):
    return jax.shard_map(
        per_device,
        mesh=mesh,
        in_specs=(
            P("el", "az", None),
            P("el", "az", None),
            P("az", "el", None, None),
            P("az", "el", None, None, None),
            P("el", "az", None),
            P(),
            P(),
            P(),
            P(),
            P(),
            P(),
            P(),
            P(),
        ),
        out_specs=P("el", "az", None),
        check_vma=False,
    )
```

time: 140 us -> 36 us (0.26)
  the two profiles are of different devices: /device:TPU:24 before, /device:TPU:6 now
where the time goes in v1:
time: 36 us; the launch traced here: 35.8 us
  Pallas kernels  32.5 us (90%)
  local copies, waits for them, and re-layouts  3.26 us (9%)
    pallas_call x1, Pallas kernels, per_device(): pl.pallas_call(kernel, out_shape=jax.ShapeDtypeStruct((2, COLS, D), BF16)...  32.5 us
    unnamed x2, local copies, waits for them, and re-layouts  3.26 us

profile of v1, /device:TPU:6, one launch (start us, length us, event | category | flops | bytes accessed | tf_op | source)
XLA Modules:
  0.0 35.8 jit_solution(11201352194937076971)
XLA Ops:
  0.0 1.6 %copy.14.index_hbm = s32[2,256,16]{2,1,0:T(8,128)} copy(s32[2,256,16]{1,2,0:T(8,128)} %param.17) | data formatting | bytes 65536 | tf_op args[4]
  1.6 32.5 %decoder.1 = bf16[2,256,256]{2,1,0:T(8,128)(2,1)} custom-call(bf16[2,256,256]{2,1,0:T(8,128)(2,1)} %points_hbm.1, bf16[2,256,256]{2,1,0:T(8,128)(2,1)} %skip_hbm.1, bf16[1,1,128,256]{3,2,1,0:T(8,128)(2,1)} %tokens_hbm.1, s32[1,1,5,8,16]{4,3,2,1,0:T(8,128)} %slots_hbm.1, s32[2,256,16]{2,1,0:T(8,128)} %copy.14.index_hbm, bf16[256,256]{1,0:T(8,128)(2,1)} %wq_hbm.1, ...), custom_call_target="tpu_custom_call" | custom-call | tf_op jit(solution)/shard_map/decoder/pallas_call | solution.py:408
  34.1 1.7 %copy.16 = bf16[2,256,256]{2,1,0:T(8,128)(2,1)} copy(bf16[2,256,256]{2,1,0:T(8,128)(2,1)} %decoder.1) | data formatting | bytes 524288

commit v2 on v1

--- a/solution.py
+++ b/solution.py
@@ -119,15 +119,14 @@
     slt_in = load(1, slots_hbm.at[0, 0], slt)
     wq_in = load(2, wq_hbm, wq)
     pts_in = []
-    idx_in = []
     skp_in = []
     for number, (chunk, row, col, width, place) in enumerate(SEGMENTS):
         here = pl.ds(chunk * HALF + place, width)
         pts_in.append(load(3 + number, points_hbm.at[row, pl.ds(col, width)], pts.at[here]))
-        idx_in.append(load(9 + number, index_hbm.at[row, pl.ds(col, width)], idx.at[here]))
     for number, (chunk, row, col, width, place) in enumerate(SEGMENTS):
         here = pl.ds(chunk * HALF + place, width)
         skp_in.append(load(15 + number, skip_hbm.at[row, pl.ds(col, width)], skp.at[here]))
+    idx_in = load(9, index_hbm, idx)
     ws_in = load(21, ws_hbm, ws)
     wk_in = load(22, wk_hbm, wk)
     wv_in = load(23, wv_hbm, wv)
@@ -206,11 +205,12 @@
                 token_copy(j, r).start()
     recv[REACH * EL + el] = payload[REACH * EL + el]
 
-    for copy in idx_in:
-        copy.wait()
-    entries = idx[...]
-    low = nt(eye, (entries & (TOK - 1)).astype(F32).astype(BF16)).astype(jnp.int32)
-    high = nt(eye, lax.shift_right_logical(entries, 7).astype(F32).astype(BF16)).astype(jnp.int32)
+    idx_in.wait()
+    entries = jnp.concatenate(
+        [idx[row, :, col : col + width] for _, row, col, width, _ in SEGMENTS], axis=1
+    )
+    low = entries & (TOK - 1)
+    high = lax.shift_right_logical(entries, 7)
     unit = lax.shift_left(jnp.ones_like(high), high * 5)
 
     down = lax.broadcasted_iota(jnp.int32, (8, POINTS), 0)
@@ -404,6 +404,7 @@
 
 
 def per_device(*args):
+    args = args[:4] + (jnp.swapaxes(args[4], 1, 2),) + args[5:]
     any_spec = pl.BlockSpec(memory_space=pl.ANY)
     return pl.pallas_call(
         kernel,
@@ -415,7 +416,7 @@
             pltpu.VMEM((POINTS, D), BF16),
             pltpu.VMEM((TOK, D), BF16),
             pltpu.VMEM((OFFSETS, EL, CAP), jnp.int32),
-            pltpu.VMEM((POINTS, NEAR), jnp.int32),
+            pltpu.VMEM((2, NEAR, COLS), jnp.int32),
             pltpu.VMEM((D, D), BF16),
             pltpu.VMEM((D, D), BF16),
             pltpu.VMEM((D, D), BF16),

time: 36 us -> 34.3 us (0.953)
  local copies, waits for them, and re-layouts: 3.26 us -> 1.67 us
    unnamed x2 -> x1, local copies, waits for them, and re-layouts: 3.26 us -> 1.67 us
where the time goes in v2:
time: 34.3 us; the launch traced here: 34.2 us
  Pallas kernels  32.5 us (95%)
  local copies, waits for them, and re-layouts  1.67 us (5%)
    pallas_call x1, Pallas kernels, per_device(): pl.pallas_call(kernel, out_shape=jax.ShapeDtypeStruct((2, COLS, D), BF16)...  32.5 us
    unnamed x1, local copies, waits for them, and re-layouts  1.67 us

profile of v2, /device:TPU:6, one launch (start us, length us, event | category | flops | bytes accessed | tf_op | source)
XLA Modules:
  0.0 34.2 jit_solution(12566850607109111082)
XLA Ops:
  0.0 32.5 %decoder.1 = bf16[2,256,256]{2,1,0:T(8,128)(2,1)} custom-call(bf16[2,256,256]{2,1,0:T(8,128)(2,1)} %points_hbm.1, bf16[2,256,256]{2,1,0:T(8,128)(2,1)} %skip_hbm.1, bf16[1,1,128,256]{3,2,1,0:T(8,128)(2,1)} %tokens_hbm.1, s32[1,1,5,8,16]{4,3,2,1,0:T(8,128)} %slots_hbm.1, s32[2,16,256]{2,1,0:T(8,128)} %bitcast.1, bf16[256,256]{1,0:T(8,128)(2,1)} %wq_hbm.1, ...), custom_call_target="tpu_custom_call" | custom-call | tf_op jit(solution)/shard_map/decoder/pallas_call | solution.py:409
  32.5 1.7 %copy.15 = bf16[2,256,256]{2,1,0:T(8,128)(2,1)} copy(bf16[2,256,256]{2,1,0:T(8,128)(2,1)} %decoder.1) | data formatting | bytes 524288

commit v3 on v2

v3 whole, which is shorter than its diff:
```python
import math

import jax
import jax.numpy as jnp
from jax import lax
from jax.experimental import pallas as pl
from jax.experimental.pallas import tpu as pltpu
from jax.sharding import PartitionSpec as P

D = 256
HEADS = 8
HEAD = D // HEADS
FF = 1024
NEAR = 16
REACH = 2
OFFSETS = 5
CAP = 16
TOK = 128
COLS = 256
EL = 8
AZ = 16
SLOTS = OFFSETS * EL
POINTS = 512
HALF = 256
PAD = 16
FAR = -1e30
GELU_IN = math.sqrt(2.0 / math.pi)
GELU_CUBE = 0.044715 * GELU_IN
MESH = pl.DeviceIdType.MESH
BF16 = jnp.bfloat16
F32 = jnp.float32

RANK = (0, 1, 4, 6, 3, 7, 5, 2)
BLOCKS = 8
GROUPS = SLOTS // BLOCKS
SPAN = BLOCKS * CAP
LAG = 8
OWN = RANK[0] * OFFSETS + REACH
SEND_ORDER = (0, 1, 7, 4, 2, 6, 3, 5)

SEGMENTS = (
    (0, 0, 0, 64, 0),
    (0, 0, 192, 64, 64),
    (0, 1, 0, 64, 128),
    (0, 1, 192, 64, 192),
    (1, 0, 64, 128, 0),
    (1, 1, 64, 128, 128),
)


def nt(a, b):
    return lax.dot_general(a, b, (((1,), (1,)), ((), ())), preferred_element_type=F32)


def nn(a, b):
    return lax.dot_general(a, b, (((1,), (0,)), ((), ())), preferred_element_type=F32)


def inv_rms(x):
    return lax.rsqrt(jnp.mean(x * x, axis=-1, keepdims=True) + 1e-06)


def gelu(u):
    half = 0.5 * u
    return half + half * jnp.tanh(u * (GELU_IN + GELU_CUBE * (u * u)))


def kernel(
    points_hbm,
    skip_hbm,
    tokens_hbm,
    slots_hbm,
    index_hbm,
    wq_hbm,
    wk_hbm,
    wv_hbm,
    wo_hbm,
    wh_hbm,
    ws_hbm,
    wd_hbm,
    wc_hbm,
    out_ref,
    pts,
    skp,
    tok,
    slt,
    idx,
    wq,
    wk,
    wv,
    wo,
    wh,
    ws,
    wd,
    wc,
    payload,
    recv,
    qmt,
    hs,
    bias,
    kbuf,
    vt,
    acc,
    best,
    scores,
    att,
    joined,
    cin,
    wvt,
    in_sem,
    send_sem,
    recv_sem,
    halo_send,
    halo_recv,
):
    az = lax.axis_index("az")
    el = lax.axis_index("el")

    def az_at(step):
        return lax.rem(az + step + AZ, AZ)

    def el_at(step):
        return lax.rem(el + step, EL)

    def load(number, src, dst):
        copy = pltpu.make_async_copy(src, dst, in_sem.at[number])
        copy.start()
        return copy

    tok_in = load(0, tokens_hbm.at[0, 0], tok)
    slt_in = load(1, slots_hbm.at[0, 0], slt)

    barrier = pltpu.get_barrier_semaphore()
    for r in range(EL):
        for j in range(OFFSETS):
            if (j, r) != (REACH, 0):
                pl.semaphore_signal(
                    barrier,
                    inc=1,
                    device_id={"az": az_at(j - REACH), "el": el_at(r)},
                    device_id_type=MESH,
                )

    wq_in = load(2, wq_hbm, wq)
    pts_in = []
    skp_in = []
    for number, (chunk, row, col, width, place) in enumerate(SEGMENTS):
        here = pl.ds(chunk * HALF + place, width)
        pts_in.append(load(3 + number, points_hbm.at[row, pl.ds(col, width)], pts.at[here]))
    idx_in = load(9, index_hbm, idx)
    wv_in = load(23, wv_hbm, wv)
    wk_in = load(22, wk_hbm, wk)

    slt_in.wait()
    tok_in.wait()
    eye = (
        lax.broadcasted_iota(jnp.int32, (NEAR, NEAR), 0)
        == lax.broadcasted_iota(jnp.int32, (NEAR, NEAR), 1)
    ).astype(F32).astype(BF16)
    slot_cols = nt(eye, slt[...].reshape(SLOTS, CAP).astype(F32).astype(BF16))
    lane_id = lax.broadcasted_iota(jnp.int32, (CAP, TOK), 1).astype(F32)
    picks = jnp.concatenate(
        [
            (jnp.broadcast_to(slot_cols[:, s : s + 1], (CAP, TOK)) == lane_id)
            .astype(F32)
            .astype(BF16)
            for s in range(SLOTS)
        ],
        axis=0,
    )
    payload[...] = nn(picks, tok[...]).astype(BF16).reshape(SLOTS, CAP, D)

    pl.semaphore_wait(barrier, SLOTS - 1)

    def token_copy(j, r):
        f = el_at(r)
        place = RANK[(EL - r) % EL] * OFFSETS + j
        return pltpu.make_async_remote_copy(
            src_ref=payload.at[j * EL + f],
            dst_ref=recv.at[place],
            send_sem=send_sem.at[place],
            recv_sem=recv_sem.at[place],
            device_id={"az": az_at(j - REACH), "el": f},
            device_id_type=MESH,
        )

    for r in SEND_ORDER:
        for j in range(OFFSETS):
            if (j, r) != (REACH, 0):
                token_copy(j, r).start()
    recv[OWN] = payload[REACH * EL + el]

    for number, (chunk, row, col, width, place) in enumerate(SEGMENTS):
        here = pl.ds(chunk * HALF + place, width)
        skp_in.append(load(15 + number, skip_hbm.at[row, pl.ds(col, width)], skp.at[here]))
    ws_in = load(21, ws_hbm, ws)
    wo_in = load(24, wo_hbm, wo)
    wh_in = load(25, wh_hbm, wh)
    wd_in = load(26, wd_hbm, wd)
    wc_in = load(27, wc_hbm, wc)

    wq_in.wait()
    for copy in pts_in:
        copy.wait()
    query_t = (nt(wq[...].T, pts[...]) * (1.0 / math.sqrt(HEAD) / math.log(2.0))).astype(BF16)
    zero_rows = jnp.zeros((HEAD, POINTS), BF16)
    for h in range(HEADS):
        for part in range(4):
            rows = pl.ds(part * HEAD, HEAD)
            if part == h % 4:
                qmt[h, rows, :] = query_t[h * HEAD : (h + 1) * HEAD, :]
            else:
                qmt[h, rows, :] = zero_rows

    idx_in.wait()
    named = jnp.concatenate(
        [idx[row, :, col : col + width] for _, row, col, width, _ in SEGMENTS], axis=1
    )
    away = (lax.shift_right_logical(named, 4) - el) & (EL - 1)
    ranks = jnp.full_like(named, sum(rank << (3 * r) for r, rank in enumerate(RANK)))
    ranks = lax.shift_right_logical(ranks, away * 3) & (EL - 1)
    entries = (ranks * OFFSETS + lax.shift_right_logical(named, 7)) * CAP + (named & (CAP - 1))
    low = entries & (SPAN - 1)
    high = lax.shift_right_logical(entries, 7)
    unit = lax.shift_left(jnp.ones_like(high), high * 5)

    down = lax.broadcasted_iota(jnp.int32, (8, POINTS), 0)
    for block in range(SPAN // 8):
        total = jnp.zeros((8, POINTS), jnp.int32)
        for n in range(NEAR):
            hit = jnp.broadcast_to(low[n : n + 1, :] - block * 8, (8, POINTS)) == down
            total = total + jnp.where(hit, jnp.broadcast_to(unit[n : n + 1, :], (8, POINTS)), 0)
        for group in range(GROUPS):
            count = lax.shift_right_logical(total, 5 * group) & 31
            logs = jnp.log(count.astype(F32)) * (1.0 / math.log(2.0))
            bias[group, pl.ds(block * 8, 8), :] = jnp.where(count > 0, logs, FAR)

    wv_in.wait()
    wvt[...] = wv[...].T
    for group in range(GROUPS):
        vt[group, :, pl.ds(HEAD, 16), :] = jnp.ones((HEADS, 16, SPAN), BF16)

    @pl.when(el == 0)
    def _():
        cin[0, :, :] = jnp.zeros((COLS + 2 * PAD, D), BF16)

    @pl.when(el == EL - 1)
    def _():
        cin[3, :, :] = jnp.zeros((COLS + 2 * PAD, D), BF16)

    wk_in.wait()

    def project(group):
        for place in range(group * BLOCKS, (group + 1) * BLOCKS):
            if place != OWN:
                rank, j = divmod(place, OFFSETS)
                token_copy(j, (EL - RANK.index(rank)) % EL).wait_recv()
        rows = recv[pl.ds(group * BLOCKS, BLOCKS)].reshape(SPAN, D)
        kbuf[group] = nn(rows, wk[...]).astype(BF16)
        wide = rows.astype(F32)
        normed_tokens = (wide * inv_rms(wide)).astype(BF16)
        value_t = nt(wvt[...], normed_tokens).astype(BF16)
        for h in range(HEADS):
            vt[group, h, pl.ds(0, HEAD), :] = value_t[h * HEAD : (h + 1) * HEAD, :]

    def attend(group, chunks):
        tasks = [(chunk, h) for chunk in chunks for h in range(HEADS)]
        tops = {}
        for step in range(len(tasks) + LAG):
            if step < len(tasks):
                chunk, h = tasks[step]
                span = pl.ds(chunk * HALF, HALF)
                lanes = pl.ds((h // 4) * 128, 128)
                raw = nn(kbuf[group, :, lanes], qmt[h, :, span]) + bias[group, :, span]
                scores[step % (LAG + 1)] = raw
                top = jnp.max(raw, axis=0, keepdims=True)
                tops[step] = (top, None)
                if group > 0:
                    old = best[chunk, h][:1, :]
                    top = jnp.maximum(old, top)
                    tops[step] = (top, jnp.exp2(old - top))
                if group < GROUPS - 1:
                    best[chunk, h] = jnp.broadcast_to(top, (8, HALF))
            if step >= LAG:
                chunk, h = tasks[step - LAG]
                top, fade = tops.pop(step - LAG)
                weights = jnp.exp2((scores[(step - LAG) % (LAG + 1)] - top).astype(BF16))
                summed = nn(vt[group, h], weights)[: HEAD + 8, :]
                if group > 0:
                    summed = summed + acc[chunk, h] * fade
                acc[chunk, h] = summed

    def halo(number, src, dst, device):
        return pltpu.make_async_remote_copy(
            src_ref=src,
            dst_ref=dst,
            send_sem=halo_send.at[number],
            recv_sem=halo_recv.at[number],
            device_id=device,
            device_id_type=MESH,
        )

    west, east = az_at(-1), az_at(1)
    above = jnp.maximum(el - 1, 0)
    below = jnp.minimum(el + 1, EL - 1)
    first, last = pl.ds(PAD, PAD), pl.ds(COLS, PAD)
    left_pad, right_pad = pl.ds(0, PAD), pl.ds(PAD + COLS, PAD)

    def row_copies(chunk, row):
        number = 5 * row
        mine, theirs = (1, 3) if row == 0 else (2, 0)
        there = above if row == 0 else below
        if chunk == 1:
            mid = pl.ds(PAD + 64, 128)
            return [halo(number, cin.at[mine, mid], cin.at[theirs, mid], {"az": az, "el": there})]
        one, two = pl.ds(PAD, 64), pl.ds(PAD + 192, 64)
        return [
            halo(number + 1, cin.at[mine, one], cin.at[theirs, one], {"az": az, "el": there}),
            halo(number + 2, cin.at[mine, two], cin.at[theirs, two], {"az": az, "el": there}),
            halo(
                number + 3, cin.at[mine, first], cin.at[theirs, right_pad], {"az": west, "el": there}
            ),
            halo(
                number + 4, cin.at[mine, last], cin.at[theirs, left_pad], {"az": east, "el": there}
            ),
        ]

    def side_copies():
        return [
            halo(10, cin.at[1, first], cin.at[1, right_pad], {"az": west, "el": el}),
            halo(11, cin.at[2, first], cin.at[2, right_pad], {"az": west, "el": el}),
            halo(12, cin.at[1, last], cin.at[1, left_pad], {"az": east, "el": el}),
            halo(13, cin.at[2, last], cin.at[2, left_pad], {"az": east, "el": el}),
        ]

    def sends_row(row):
        return (el > 0) if row == 0 else (el < EL - 1)

    def join(chunk):
        for h in range(HEADS):
            share = acc[chunk, h, :HEAD, :] * (1.0 / acc[chunk, h, HEAD : HEAD + 1, :])
            att[pl.ds(h * HEAD, HEAD), :] = share.astype(BF16)
        attended = att[...].T
        for row in range(2):
            span = pl.ds(chunk * HALF + row * 128, 128)
            residual = pts[span, :].astype(F32) + nn(
                attended[row * 128 : (row + 1) * 128, :], wo[...]
            )
            normed = (residual * inv_rms(residual)).astype(BF16)
            total = residual
            for block in range(FF // D):
                cols = pl.ds(block * D, D)
                hidden = gelu(nn(normed, wh[:, cols]) + hs[span, cols]).astype(BF16)
                total = total + nn(hidden, wd[cols, :])
            conv_in = (total * inv_rms(total)).astype(BF16)
            for c, at_row, col, width, place in SEGMENTS:
                if (c, at_row) == (chunk, row):
                    start = place - row * 128
                    joined[row, pl.ds(col, width), :] = total[start : start + width, :]
                    cin[1 + row, pl.ds(PAD + col, width), :] = conv_in[start : start + width, :]

            @pl.when(sends_row(row))
            def _():
                for copy in row_copies(chunk, row):
                    copy.start()

        if chunk == 0:
            for copy in side_copies():
                copy.start()

    for group in range(2):
        project(group)
        attend(group, (0, 1))

    for copy in skp_in:
        copy.wait()
    ws_in.wait()
    for block in range(FF // D):
        cols = pl.ds(block * D, D)
        hs[:, cols] = nn(skp[...], ws[:, cols])

    for group in range(2, GROUPS - 1):
        project(group)
        attend(group, (0, 1))

    wo_in.wait()
    wh_in.wait()
    wd_in.wait()
    project(GROUPS - 1)
    for chunk in range(2):
        attend(GROUPS - 1, (chunk,))
        join(chunk)

    for copy in side_copies():
        copy.wait_recv()
    wc_in.wait()

    def taps(row):
        return [cin[row, pl.ds(PAD + step, COLS), :] for step in (-1, 0, 1)]

    own = jnp.concatenate(taps(1) + taps(2), axis=1)
    joined[0] = joined[0] + nn(own, wc[pl.ds(3, 6)].reshape(6 * D, D))
    joined[1] = joined[1] + nn(own, wc[pl.ds(0, 6)].reshape(6 * D, D))

    for j in range(OFFSETS):
        for r in range(EL):
            if (j, r) != (REACH, 0):
                token_copy(j, r).wait_send()
    for copy in side_copies():
        copy.wait_send()

    for row in range(2):

        @pl.when(sends_row(row))
        def _():
            for chunk in range(2):
                for copy in row_copies(chunk, row):
                    copy.wait_send()

    @pl.when(el > 0)
    def _():
        for chunk in range(2):
            for copy in row_copies(chunk, 1):
                copy.wait_recv()

    upper = nn(jnp.concatenate(taps(0), axis=1), wc[pl.ds(0, 3)].reshape(3 * D, D))
    out_ref[0] = (joined[0] + upper).astype(BF16)

    @pl.when(el < EL - 1)
    def _():
        for chunk in range(2):
            for copy in row_copies(chunk, 0):
                copy.wait_recv()

    lower = nn(jnp.concatenate(taps(3), axis=1), wc[pl.ds(6, 3)].reshape(3 * D, D))
    out_ref[1] = (joined[1] + lower).astype(BF16)


def per_device(*args):
    args = args[:4] + (jnp.swapaxes(args[4], 1, 2),) + args[5:]
    any_spec = pl.BlockSpec(memory_space=pl.ANY)
    return pl.pallas_call(
        kernel,
        out_shape=pltpu.VMEM((2, COLS, D), BF16),
        in_specs=[any_spec] * len(args),
        out_specs=pl.BlockSpec(memory_space=pltpu.VMEM),
        scratch_shapes=[
            pltpu.VMEM((POINTS, D), BF16),
            pltpu.VMEM((POINTS, D), BF16),
            pltpu.VMEM((TOK, D), BF16),
            pltpu.VMEM((OFFSETS, EL, CAP), jnp.int32),
            pltpu.VMEM((2, NEAR, COLS), jnp.int32),
            pltpu.VMEM((D, D), BF16),
            pltpu.VMEM((D, D), BF16),
            pltpu.VMEM((D, D), BF16),
            pltpu.VMEM((D, D), BF16),
            pltpu.VMEM((D, FF), BF16),
            pltpu.VMEM((D, FF), BF16),
            pltpu.VMEM((FF, D), BF16),
            pltpu.VMEM((9, D, D), BF16),
            pltpu.VMEM((SLOTS, CAP, D), BF16),
            pltpu.VMEM((SLOTS, CAP, D), BF16),
            pltpu.VMEM((HEADS, D // 2, POINTS), BF16),
            pltpu.VMEM((POINTS, FF), F32),
            pltpu.VMEM((GROUPS, SPAN, POINTS), F32),
            pltpu.VMEM((GROUPS, SPAN, D), BF16),
            pltpu.VMEM((GROUPS, HEADS, HEAD + 16, SPAN), BF16),
            pltpu.VMEM((2, HEADS, HEAD + 8, HALF), F32),
            pltpu.VMEM((2, HEADS, 8, HALF), F32),
            pltpu.VMEM((LAG + 1, SPAN, HALF), F32),
            pltpu.VMEM((D, HALF), BF16),
            pltpu.VMEM((2, COLS, D), F32),
            pltpu.VMEM((4, COLS + 2 * PAD, D), BF16),
            pltpu.VMEM((D, D), BF16),
            pltpu.SemaphoreType.DMA((28,)),
            pltpu.SemaphoreType.DMA((SLOTS,)),
            pltpu.SemaphoreType.DMA((SLOTS,)),
            pltpu.SemaphoreType.DMA((14,)),
            pltpu.SemaphoreType.DMA((14,)),
        ],
        compiler_params=pltpu.CompilerParams(
            collective_id=0, has_side_effects=True, vmem_limit_bytes=56 * 1024 * 1024
        ),
        name="decoder",
    )(*args)


def solution(mesh):
    return jax.shard_map(
        per_device,
        mesh=mesh,
        in_specs=(
            P("el", "az", None),
            P("el", "az", None),
            P("az", "el", None, None),
            P("az", "el", None, None, None),
            P("el", "az", None),
            P(),
            P(),
            P(),
            P(),
            P(),
            P(),
            P(),
            P(),
        ),
        out_specs=P("el", "az", None),
        check_vma=False,
    )
```

time: 34.3 us -> 29.8 us (0.87); the launches traced: 34.2 us -> 29.3 us
  Pallas kernels: 32.5 us -> 28.6 us
  local copies, waits for them, and re-layouts: 1.67 us -> 0.71 us
    pallas_call x1, Pallas kernels: 32.5 us -> 28.6 us  [per_device(): pl.pallas_call(kernel, out_shape=pltpu.VMEM((2, COLS, D), BF16), in_specs...]
    unnamed x1, local copies, waits for them, and re-layouts: 1.67 us -> 0.71 us
where the time goes in v3:
time: 29.8 us; the launch traced here: 29.3 us
  Pallas kernels  28.6 us (96%)
  local copies, waits for them, and re-layouts  0.71 us (2%)
    pallas_call x1, Pallas kernels, per_device(): pl.pallas_call(kernel, out_shape=pltpu.VMEM((2, COLS, D), BF16), in_specs...  28.6 us
    unnamed x1, local copies, waits for them, and re-layouts  0.71 us

profile of v3, /device:TPU:6, one launch (start us, length us, event | category | flops | bytes accessed | tf_op | source)
XLA Modules:
  0.0 29.3 jit_solution(9554726730122794204)
XLA Ops:
  0.0 28.6 %decoder.1 = bf16[2,256,256]{2,1,0:T(8,128)(2,1)S(1)} custom-call(bf16[2,256,256]{2,1,0:T(8,128)(2,1)} %points_hbm.1, bf16[2,256,256]{2,1,0:T(8,128)(2,1)} %skip_hbm.1, bf16[1,1,128,256]{3,2,1,0:T(8,128)(2,1)} %tokens_hbm.1, s32[1,1,5,8,16]{4,3,2,1,0:T(8,128)} %slots_hbm.1, s32[2,16,256]{2,1,0:T(8,128)} %bitcast.1, bf16[256,256]{1,0:T(8,128)(2,1)} %wq_hbm.1, ...), custom_call_target="tpu_custom_call" | custom-call | tf_op jit(solution)/shard_map/decoder/pallas_call | solution.py:442
  28.6 0.7 %copy.15 = bf16[2,256,256]{2,1,0:T(8,128)(2,1)} copy(bf16[2,256,256]{2,1,0:T(8,128)(2,1)S(1)} %decoder.1) | data formatting | bytes 524288

commit v4 on v3

--- a/solution.py
+++ b/solution.py
@@ -35,6 +35,7 @@
 GROUPS = SLOTS // BLOCKS
 SPAN = BLOCKS * CAP
 LAG = 8
+SKIP_GROUP = 1
 OWN = RANK[0] * OFFSETS + REACH
 SEND_ORDER = (0, 1, 7, 4, 2, 6, 3, 5)
 
@@ -61,8 +62,8 @@
 
 
 def gelu(u):
-    half = 0.5 * u
-    return half + half * jnp.tanh(u * (GELU_IN + GELU_CUBE * (u * u)))
+    half = BF16(0.5) * u
+    return half + half * jnp.tanh(u * (BF16(GELU_IN) + BF16(GELU_CUBE) * (u * u)))
 
 
 def kernel(
@@ -232,8 +233,7 @@
             total = total + jnp.where(hit, jnp.broadcast_to(unit[n : n + 1, :], (8, POINTS)), 0)
         for group in range(GROUPS):
             count = lax.shift_right_logical(total, 5 * group) & 31
-            logs = jnp.log(count.astype(F32)) * (1.0 / math.log(2.0))
-            bias[group, pl.ds(block * 8, 8), :] = jnp.where(count > 0, logs, FAR)
+            bias[group, pl.ds(block * 8, 8), :] = jnp.maximum(jnp.log2(count.astype(F32)), FAR)
 
     wv_in.wait()
     wvt[...] = wv[...].T
@@ -263,32 +263,33 @@
         for h in range(HEADS):
             vt[group, h, pl.ds(0, HEAD), :] = value_t[h * HEAD : (h + 1) * HEAD, :]
 
-    def attend(group, chunks):
-        tasks = [(chunk, h) for chunk in chunks for h in range(HEADS)]
-        tops = {}
-        for step in range(len(tasks) + LAG):
-            if step < len(tasks):
-                chunk, h = tasks[step]
-                span = pl.ds(chunk * HALF, HALF)
-                lanes = pl.ds((h // 4) * 128, 128)
-                raw = nn(kbuf[group, :, lanes], qmt[h, :, span]) + bias[group, :, span]
-                scores[step % (LAG + 1)] = raw
-                top = jnp.max(raw, axis=0, keepdims=True)
-                tops[step] = (top, None)
-                if group > 0:
-                    old = best[chunk, h][:1, :]
-                    top = jnp.maximum(old, top)
-                    tops[step] = (top, jnp.exp2(old - top))
-                if group < GROUPS - 1:
-                    best[chunk, h] = jnp.broadcast_to(top, (8, HALF))
-            if step >= LAG:
-                chunk, h = tasks[step - LAG]
-                top, fade = tops.pop(step - LAG)
-                weights = jnp.exp2((scores[(step - LAG) % (LAG + 1)] - top).astype(BF16))
-                summed = nn(vt[group, h], weights)[: HEAD + 8, :]
-                if group > 0:
-                    summed = summed + acc[chunk, h] * fade
-                acc[chunk, h] = summed
+    pending = []
+    begun = [0]
+
+    def begin(group, chunk, h):
+        span = pl.ds(chunk * HALF, HALF)
+        lanes = pl.ds((h // 4) * 128, 128)
+        slot = begun[0] % (LAG + 1)
+        begun[0] += 1
+        raw = nn(kbuf[group, :, lanes], qmt[h, :, span]) + bias[group, :, span]
+        scores[slot] = raw
+        top = jnp.max(raw, axis=0, keepdims=True)
+        fade = None
+        if group > 0:
+            old = best[chunk, h][:1, :]
+            top = jnp.maximum(old, top)
+            fade = jnp.exp2(old - top)
+        if group < GROUPS - 1:
+            best[chunk, h] = jnp.broadcast_to(top, (8, HALF))
+        pending.append((group, chunk, h, slot, top, fade))
+
+    def finish():
+        group, chunk, h, slot, top, fade = pending.pop(0)
+        weights = jnp.exp2((scores[slot] - top).astype(BF16))
+        summed = nn(vt[group, h], weights)[: HEAD + 8, :]
+        if group > 0:
+            summed = summed + acc[chunk, h] * fade
+        acc[chunk, h] = summed
 
     def halo(number, src, dst, device):
         return pltpu.make_async_remote_copy(
@@ -341,7 +342,7 @@
             share = acc[chunk, h, :HEAD, :] * (1.0 / acc[chunk, h, HEAD : HEAD + 1, :])
             att[pl.ds(h * HEAD, HEAD), :] = share.astype(BF16)
         attended = att[...].T
-        for row in range(2):
+        for row in (1, 0):
             span = pl.ds(chunk * HALF + row * 128, 128)
             residual = pts[span, :].astype(F32) + nn(
                 attended[row * 128 : (row + 1) * 128, :], wo[...]
@@ -350,7 +351,7 @@
             total = residual
             for block in range(FF // D):
                 cols = pl.ds(block * D, D)
-                hidden = gelu(nn(normed, wh[:, cols]) + hs[span, cols]).astype(BF16)
+                hidden = gelu((nn(normed, wh[:, cols]) + hs[span, cols]).astype(BF16))
                 total = total + nn(hidden, wd[cols, :])
             conv_in = (total * inv_rms(total)).astype(BF16)
             for c, at_row, col, width, place in SEGMENTS:
@@ -359,6 +360,9 @@
                     joined[row, pl.ds(col, width), :] = total[start : start + width, :]
                     cin[1 + row, pl.ds(PAD + col, width), :] = conv_in[start : start + width, :]
 
+            for _ in range(min(HEADS // 2, len(pending))):
+                finish()
+
             @pl.when(sends_row(row))
             def _():
                 for copy in row_copies(chunk, row):
@@ -368,28 +372,37 @@
             for copy in side_copies():
                 copy.start()
 
-    for group in range(2):
-        project(group)
-        attend(group, (0, 1))
-
-    for copy in skp_in:
-        copy.wait()
-    ws_in.wait()
-    for block in range(FF // D):
+    def skip_part(block):
         cols = pl.ds(block * D, D)
         hs[:, cols] = nn(skp[...], ws[:, cols])
 
-    for group in range(2, GROUPS - 1):
+    for group in range(GROUPS - 1):
         project(group)
-        attend(group, (0, 1))
+        if group == SKIP_GROUP:
+            for copy in skp_in:
+                copy.wait()
+            ws_in.wait()
+        for chunk in range(2):
+            for h in range(HEADS):
+                begin(group, chunk, h)
+                if len(pending) > LAG:
+                    finish()
+                if group == SKIP_GROUP and h % 4 == 3:
+                    skip_part(2 * chunk + h // 4)
+    while pending:
+        finish()
 
     wo_in.wait()
     wh_in.wait()
     wd_in.wait()
     project(GROUPS - 1)
     for chunk in range(2):
-        attend(GROUPS - 1, (chunk,))
-        join(chunk)
+        for h in range(HEADS):
+            begin(GROUPS - 1, chunk, h)
+            if chunk == 1:
+                finish()
+    join(0)
+    join(1)
 
     for copy in side_copies():
         copy.wait_recv()

time: 29.8 us -> 27.5 us (0.923)
  the two profiles are of different devices: /device:TPU:6 before, /device:TPU:4 now
where the time goes in v4:
time: 27.5 us; the launch traced here: 27.3 us
  Pallas kernels  26.6 us (97%)
  local copies, waits for them, and re-layouts  0.71 us (3%)
    pallas_call x1, Pallas kernels, per_device(): pl.pallas_call(kernel, out_shape=pltpu.VMEM((2, COLS, D), BF16), in_specs...  26.6 us
    unnamed x1, local copies, waits for them, and re-layouts  0.71 us

profile of v4, /device:TPU:4, one launch (start us, length us, event | category | flops | bytes accessed | tf_op | source)
XLA Modules:
  0.0 27.3 jit_solution(1029265634938082729)
XLA Ops:
  0.0 26.6 %decoder.1 = bf16[2,256,256]{2,1,0:T(8,128)(2,1)S(1)} custom-call(bf16[2,256,256]{2,1,0:T(8,128)(2,1)} %points_hbm.1, bf16[2,256,256]{2,1,0:T(8,128)(2,1)} %skip_hbm.1, bf16[1,1,128,256]{3,2,1,0:T(8,128)(2,1)} %tokens_hbm.1, s32[1,1,5,8,16]{4,3,2,1,0:T(8,128)} %slots_hbm.1, s32[2,16,256]{2,1,0:T(8,128)} %bitcast.1, bf16[256,256]{1,0:T(8,128)(2,1)} %wq_hbm.1, ...), custom_call_target="tpu_custom_call" | custom-call | tf_op jit(solution)/shard_map/decoder/pallas_call | solution.py:455
  26.6 0.7 %copy.15 = bf16[2,256,256]{2,1,0:T(8,128)(2,1)} copy(bf16[2,256,256]{2,1,0:T(8,128)(2,1)S(1)} %decoder.1) | data formatting | bytes 524288

commit v5 on v4

--- a/solution.py
+++ b/solution.py
@@ -30,14 +30,12 @@
 BF16 = jnp.bfloat16
 F32 = jnp.float32
 
-RANK = (0, 1, 4, 6, 3, 7, 5, 2)
-BLOCKS = 8
-GROUPS = SLOTS // BLOCKS
-SPAN = BLOCKS * CAP
+SPAN = EL * CAP
+ORDER = (2, 1, 3, 0, 4)
+FAR_FIRST = (2, 6, 3, 5, 4, 1, 7)
 LAG = 8
 SKIP_GROUP = 1
-OWN = RANK[0] * OFFSETS + REACH
-SEND_ORDER = (0, 1, 7, 4, 2, 6, 3, 5)
+OWN = REACH * EL
 
 SEGMENTS = (
     (0, 0, 0, 64, 0),
@@ -111,6 +109,7 @@
     in_sem,
     send_sem,
     recv_sem,
+    ready,
     halo_send,
     halo_recv,
 ):
@@ -131,16 +130,15 @@
     tok_in = load(0, tokens_hbm.at[0, 0], tok)
     slt_in = load(1, slots_hbm.at[0, 0], slt)
 
+    near = [(REACH, r) for r in range(1, EL)] + [(j, 0) for j in range(OFFSETS) if j != REACH]
     barrier = pltpu.get_barrier_semaphore()
-    for r in range(EL):
-        for j in range(OFFSETS):
-            if (j, r) != (REACH, 0):
-                pl.semaphore_signal(
-                    barrier,
-                    inc=1,
-                    device_id={"az": az_at(j - REACH), "el": el_at(r)},
-                    device_id_type=MESH,
-                )
+    for j, r in near:
+        pl.semaphore_signal(
+            barrier,
+            inc=1,
+            device_id={"az": az_at(j - REACH), "el": el_at(r)},
+            device_id_type=MESH,
+        )
 
     wq_in = load(2, wq_hbm, wq)
     pts_in = []
@@ -171,11 +169,9 @@
     )
     payload[...] = nn(picks, tok[...]).astype(BF16).reshape(SLOTS, CAP, D)
 
-    pl.semaphore_wait(barrier, SLOTS - 1)
-
     def token_copy(j, r):
         f = el_at(r)
-        place = RANK[(EL - r) % EL] * OFFSETS + j
+        place = j * EL + (EL - r) % EL
         return pltpu.make_async_remote_copy(
             src_ref=payload.at[j * EL + f],
             dst_ref=recv.at[place],
@@ -185,10 +181,26 @@
             device_id_type=MESH,
         )
 
-    for r in SEND_ORDER:
-        for j in range(OFFSETS):
-            if (j, r) != (REACH, 0):
-                token_copy(j, r).start()
+    def send_block(j):
+        pl.semaphore_wait(ready.at[OFFSETS - 1 - j], 1)
+        for r in FAR_FIRST:
+            token_copy(j, r).start()
+
+    pl.semaphore_wait(barrier, len(near))
+    for j in range(OFFSETS):
+        if j != REACH:
+            pl.semaphore_signal(
+                ready.at[j],
+                inc=1,
+                device_id={"az": az_at(j - REACH), "el": el},
+                device_id_type=MESH,
+            )
+    for r in FAR_FIRST:
+        token_copy(REACH, r).start()
+    for j in (3, 4, 1, 0):
+        token_copy(j, 0).start()
+    send_block(3)
+    send_block(4)
     recv[OWN] = payload[REACH * EL + el]
 
     for number, (chunk, row, col, width, place) in enumerate(SEGMENTS):
@@ -218,9 +230,7 @@
         [idx[row, :, col : col + width] for _, row, col, width, _ in SEGMENTS], axis=1
     )
     away = (lax.shift_right_logical(named, 4) - el) & (EL - 1)
-    ranks = jnp.full_like(named, sum(rank << (3 * r) for r, rank in enumerate(RANK)))
-    ranks = lax.shift_right_logical(ranks, away * 3) & (EL - 1)
-    entries = (ranks * OFFSETS + lax.shift_right_logical(named, 7)) * CAP + (named & (CAP - 1))
+    entries = (named & ~(SPAN - 1)) + away * CAP + (named & (CAP - 1))
     low = entries & (SPAN - 1)
     high = lax.shift_right_logical(entries, 7)
     unit = lax.shift_left(jnp.ones_like(high), high * 5)
@@ -231,13 +241,16 @@
         for n in range(NEAR):
             hit = jnp.broadcast_to(low[n : n + 1, :] - block * 8, (8, POINTS)) == down
             total = total + jnp.where(hit, jnp.broadcast_to(unit[n : n + 1, :], (8, POINTS)), 0)
-        for group in range(GROUPS):
+        for group in range(OFFSETS):
             count = lax.shift_right_logical(total, 5 * group) & 31
             bias[group, pl.ds(block * 8, 8), :] = jnp.maximum(jnp.log2(count.astype(F32)), FAR)
 
+    send_block(1)
+    send_block(0)
+
     wv_in.wait()
     wvt[...] = wv[...].T
-    for group in range(GROUPS):
+    for group in range(OFFSETS):
         vt[group, :, pl.ds(HEAD, 16), :] = jnp.ones((HEADS, 16, SPAN), BF16)
 
     @pl.when(el == 0)
@@ -251,11 +264,10 @@
     wk_in.wait()
 
     def project(group):
-        for place in range(group * BLOCKS, (group + 1) * BLOCKS):
-            if place != OWN:
-                rank, j = divmod(place, OFFSETS)
-                token_copy(j, (EL - RANK.index(rank)) % EL).wait_recv()
-        rows = recv[pl.ds(group * BLOCKS, BLOCKS)].reshape(SPAN, D)
+        for place in range(EL):
+            if group * EL + place != OWN:
+                token_copy(group, (EL - place) % EL).wait_recv()
+        rows = recv[pl.ds(group * EL, EL)].reshape(SPAN, D)
         kbuf[group] = nn(rows, wk[...]).astype(BF16)
         wide = rows.astype(F32)
         normed_tokens = (wide * inv_rms(wide)).astype(BF16)
@@ -275,11 +287,11 @@
         scores[slot] = raw
         top = jnp.max(raw, axis=0, keepdims=True)
         fade = None
-        if group > 0:
+        if group != ORDER[0]:
             old = best[chunk, h][:1, :]
             top = jnp.maximum(old, top)
             fade = jnp.exp2(old - top)
-        if group < GROUPS - 1:
+        if group != ORDER[-1]:
             best[chunk, h] = jnp.broadcast_to(top, (8, HALF))
         pending.append((group, chunk, h, slot, top, fade))
 
@@ -287,7 +299,7 @@
         group, chunk, h, slot, top, fade = pending.pop(0)
         weights = jnp.exp2((scores[slot] - top).astype(BF16))
         summed = nn(vt[group, h], weights)[: HEAD + 8, :]
-        if group > 0:
+        if group != ORDER[0]:
             summed = summed + acc[chunk, h] * fade
         acc[chunk, h] = summed
 
@@ -376,7 +388,7 @@
         cols = pl.ds(block * D, D)
         hs[:, cols] = nn(skp[...], ws[:, cols])
 
-    for group in range(GROUPS - 1):
+    for group in ORDER[:-1]:
         project(group)
         if group == SKIP_GROUP:
             for copy in skp_in:
@@ -395,10 +407,10 @@
     wo_in.wait()
     wh_in.wait()
     wd_in.wait()
-    project(GROUPS - 1)
+    project(ORDER[-1])
     for chunk in range(2):
         for h in range(HEADS):
-            begin(GROUPS - 1, chunk, h)
+            begin(ORDER[-1], chunk, h)
             if chunk == 1:
                 finish()
     join(0)
@@ -475,9 +487,9 @@
             pltpu.VMEM((SLOTS, CAP, D), BF16),
             pltpu.VMEM((HEADS, D // 2, POINTS), BF16),
             pltpu.VMEM((POINTS, FF), F32),
-            pltpu.VMEM((GROUPS, SPAN, POINTS), F32),
-            pltpu.VMEM((GROUPS, SPAN, D), BF16),
-            pltpu.VMEM((GROUPS, HEADS, HEAD + 16, SPAN), BF16),
+            pltpu.VMEM((OFFSETS, SPAN, POINTS), F32),
+            pltpu.VMEM((OFFSETS, SPAN, D), BF16),
+            pltpu.VMEM((OFFSETS, HEADS, HEAD + 16, SPAN), BF16),
             pltpu.VMEM((2, HEADS, HEAD + 8, HALF), F32),
             pltpu.VMEM((2, HEADS, 8, HALF), F32),
             pltpu.VMEM((LAG + 1, SPAN, HALF), F32),
@@ -488,6 +500,7 @@
             pltpu.SemaphoreType.DMA((28,)),
             pltpu.SemaphoreType.DMA((SLOTS,)),
             pltpu.SemaphoreType.DMA((SLOTS,)),
+            pltpu.SemaphoreType.REGULAR((OFFSETS,)),
             pltpu.SemaphoreType.DMA((14,)),
             pltpu.SemaphoreType.DMA((14,)),
         ],

time: 27.5 us -> 26.9 us (0.978)
  the two profiles are of different devices: /device:TPU:4 before, /device:TPU:6 now
where the time goes in v5:
time: 26.9 us; the launch traced here: 26.6 us
  Pallas kernels  25.9 us (96%)
  local copies, waits for them, and re-layouts  0.71 us (3%)
    pallas_call x1, Pallas kernels, per_device(): pl.pallas_call(kernel, out_shape=pltpu.VMEM((2, COLS, D), BF16), in_specs...  25.9 us
    unnamed x1, local copies, waits for them, and re-layouts  0.71 us

profile of v5, /device:TPU:6, one launch (start us, length us, event | category | flops | bytes accessed | tf_op | source)
XLA Modules:
  0.0 26.6 jit_solution(11390235775100304694)
XLA Ops:
  0.0 25.9 %decoder.1 = bf16[2,256,256]{2,1,0:T(8,128)(2,1)S(1)} custom-call(bf16[2,256,256]{2,1,0:T(8,128)(2,1)} %points_hbm.1, bf16[2,256,256]{2,1,0:T(8,128)(2,1)} %skip_hbm.1, bf16[1,1,128,256]{3,2,1,0:T(8,128)(2,1)} %tokens_hbm.1, s32[1,1,5,8,16]{4,3,2,1,0:T(8,128)} %slots_hbm.1, s32[2,16,256]{2,1,0:T(8,128)} %bitcast.1, bf16[256,256]{1,0:T(8,128)(2,1)} %wq_hbm.1, ...), custom_call_target="tpu_custom_call" | custom-call | tf_op jit(solution)/shard_map/decoder/pallas_call | solution.py:467
  25.9 0.7 %copy.15 = bf16[2,256,256]{2,1,0:T(8,128)(2,1)} copy(bf16[2,256,256]{2,1,0:T(8,128)(2,1)S(1)} %decoder.1) | data formatting | bytes 524288

commit v6 on v5

--- a/solution.py
+++ b/solution.py
@@ -130,15 +130,37 @@
     tok_in = load(0, tokens_hbm.at[0, 0], tok)
     slt_in = load(1, slots_hbm.at[0, 0], slt)
 
-    near = [(REACH, r) for r in range(1, EL)] + [(j, 0) for j in range(OFFSETS) if j != REACH]
+    place_z, core = lax.rem(lax.div(az, 2), 4), lax.rem(az, 2)
+    wrapped = {0: place_z == 0, 1: (place_z == 0) & (core == 0)}
+    ahead = {3: (place_z == 3) & (core == 1), 4: place_z == 3}
+
+    def device(j, r):
+        return {"az": az_at(j - REACH), "el": el_at(r)}
+
     barrier = pltpu.get_barrier_semaphore()
-    for j, r in near:
-        pl.semaphore_signal(
-            barrier,
-            inc=1,
-            device_id={"az": az_at(j - REACH), "el": el_at(r)},
-            device_id_type=MESH,
-        )
+
+    def greet(j, r):
+        pl.semaphore_signal(barrier, inc=1, device_id=device(j, r), device_id_type=MESH)
+
+    for r in range(1, EL):
+        greet(REACH, r)
+    for j in (0, 1):
+        greet(j, 0)
+
+        @pl.when(wrapped[j])
+        def _():
+            for r in range(1, EL):
+                greet(j, r)
+
+    for j in (3, 4):
+
+        @pl.when(jnp.logical_not(ahead[j]))
+        def _():
+            greet(j, 0)
+
+    heard = EL + OFFSETS - 2
+    heard = heard + sum(jnp.where(flag, EL - 1, 0) for flag in ahead.values())
+    heard = heard - sum(jnp.where(flag, 1, 0) for flag in wrapped.values())
 
     wq_in = load(2, wq_hbm, wq)
     pts_in = []
@@ -177,30 +199,56 @@
             dst_ref=recv.at[place],
             send_sem=send_sem.at[place],
             recv_sem=recv_sem.at[place],
-            device_id={"az": az_at(j - REACH), "el": f},
+            device_id=device(j, r),
             device_id_type=MESH,
         )
 
-    def send_block(j):
+    def send_block(j, extra=()):
+        for r in FAR_FIRST + extra:
+            token_copy(j, r).start()
+
+    def vouched(j):
         pl.semaphore_wait(ready.at[OFFSETS - 1 - j], 1)
-        for r in FAR_FIRST:
-            token_copy(j, r).start()
-
-    pl.semaphore_wait(barrier, len(near))
-    for j in range(OFFSETS):
-        if j != REACH:
-            pl.semaphore_signal(
-                ready.at[j],
-                inc=1,
-                device_id={"az": az_at(j - REACH), "el": el},
-                device_id_type=MESH,
-            )
+
+    def vouch(j):
+        pl.semaphore_signal(ready.at[j], inc=1, device_id=device(j, 0), device_id_type=MESH)
+
+    pl.semaphore_wait(barrier, heard)
+    for j in (3, 4):
+        vouch(j)
+    for j in (0, 1):
+
+        @pl.when(jnp.logical_not(wrapped[j]))
+        def _():
+            vouch(j)
+            token_copy(j, 0).start()
+
+    for j in (3, 4):
+        token_copy(j, 0).start()
     for r in FAR_FIRST:
         token_copy(REACH, r).start()
-    for j in (3, 4, 1, 0):
-        token_copy(j, 0).start()
-    send_block(3)
-    send_block(4)
+    for j in (3, 4):
+
+        @pl.when(jnp.logical_not(ahead[j]))
+        def _():
+            vouched(j)
+
+        send_block(j)
+    for j in (1, 0):
+
+        @pl.when(jnp.logical_not(wrapped[j]))
+        def _():
+            vouched(j)
+            send_block(j)
+
+    def send_wrapped():
+        for j in (1, 0):
+
+            @pl.when(wrapped[j])
+            def _():
+                vouched(j)
+                send_block(j, (0,))
+
     recv[OWN] = payload[REACH * EL + el]
 
     for number, (chunk, row, col, width, place) in enumerate(SEGMENTS):
@@ -245,8 +293,7 @@
             count = lax.shift_right_logical(total, 5 * group) & 31
             bias[group, pl.ds(block * 8, 8), :] = jnp.maximum(jnp.log2(count.astype(F32)), FAR)
 
-    send_block(1)
-    send_block(0)
+    send_wrapped()
 
     wv_in.wait()
     wvt[...] = wv[...].T
@@ -349,15 +396,16 @@
     def sends_row(row):
         return (el > 0) if row == 0 else (el < EL - 1)
 
-    def join(chunk):
+    def join(chunk, parts):
         for h in range(HEADS):
             share = acc[chunk, h, :HEAD, :] * (1.0 / acc[chunk, h, HEAD : HEAD + 1, :])
             att[pl.ds(h * HEAD, HEAD), :] = share.astype(BF16)
         attended = att[...].T
-        for row in (1, 0):
-            span = pl.ds(chunk * HALF + row * 128, 128)
+        for rows in parts:
+            begin_at, size = min(rows) * 128, len(rows) * 128
+            span = pl.ds(chunk * HALF + begin_at, size)
             residual = pts[span, :].astype(F32) + nn(
-                attended[row * 128 : (row + 1) * 128, :], wo[...]
+                attended[begin_at : begin_at + size, :], wo[...]
             )
             normed = (residual * inv_rms(residual)).astype(BF16)
             total = residual
@@ -366,19 +414,19 @@
                 hidden = gelu((nn(normed, wh[:, cols]) + hs[span, cols]).astype(BF16))
                 total = total + nn(hidden, wd[cols, :])
             conv_in = (total * inv_rms(total)).astype(BF16)
-            for c, at_row, col, width, place in SEGMENTS:
-                if (c, at_row) == (chunk, row):
-                    start = place - row * 128
+            for c, row, col, width, place in SEGMENTS:
+                if c == chunk and row in rows:
+                    start = place - begin_at
                     joined[row, pl.ds(col, width), :] = total[start : start + width, :]
                     cin[1 + row, pl.ds(PAD + col, width), :] = conv_in[start : start + width, :]
-
-            for _ in range(min(HEADS // 2, len(pending))):
+            for _ in range(len(pending) * len(rows) // 2):
                 finish()
-
-            @pl.when(sends_row(row))
-            def _():
-                for copy in row_copies(chunk, row):
-                    copy.start()
+            for row in rows:
+
+                @pl.when(sends_row(row))
+                def _():
+                    for copy in row_copies(chunk, row):
+                        copy.start()
 
         if chunk == 0:
             for copy in side_copies():
@@ -413,8 +461,8 @@
             begin(ORDER[-1], chunk, h)
             if chunk == 1:
                 finish()
-    join(0)
-    join(1)
+    join(0, ((1, 0),))
+    join(1, ((1, 0),))
 
     for copy in side_copies():
         copy.wait_recv()

time: 26.9 us -> 26.6 us (0.989)
  the two profiles are of different devices: /device:TPU:6 before, /device:TPU:7 now
where the time goes in v6:
time: 26.6 us; the launch traced here: 26.4 us
  Pallas kernels  25.7 us (97%)
  local copies, waits for them, and re-layouts  0.71 us (3%)
    pallas_call x1, Pallas kernels, per_device(): pl.pallas_call(kernel, out_shape=pltpu.VMEM((2, COLS, D), BF16), in_specs...  25.7 us
    unnamed x1, local copies, waits for them, and re-layouts  0.71 us

profile of v6, /device:TPU:7, one launch (start us, length us, event | category | flops | bytes accessed | tf_op | source)
XLA Modules:
  0.0 26.4 jit_solution(7999142764992539913)
XLA Ops:
  0.0 25.7 %decoder.1 = bf16[2,256,256]{2,1,0:T(8,128)(2,1)S(1)} custom-call(bf16[2,256,256]{2,1,0:T(8,128)(2,1)} %points_hbm.1, bf16[2,256,256]{2,1,0:T(8,128)(2,1)} %skip_hbm.1, bf16[1,1,128,256]{3,2,1,0:T(8,128)(2,1)} %tokens_hbm.1, s32[1,1,5,8,16]{4,3,2,1,0:T(8,128)} %slots_hbm.1, s32[2,16,256]{2,1,0:T(8,128)} %bitcast.1, bf16[256,256]{1,0:T(8,128)(2,1)} %wq_hbm.1, ...), custom_call_target="tpu_custom_call" | custom-call | tf_op jit(solution)/shard_map/decoder/pallas_call | solution.py:515
  25.7 0.7 %copy.15 = bf16[2,256,256]{2,1,0:T(8,128)(2,1)} copy(bf16[2,256,256]{2,1,0:T(8,128)(2,1)S(1)} %decoder.1) | data formatting | bytes 524288

commit v7 on v6

--- a/solution.py
+++ b/solution.py
@@ -31,10 +31,9 @@
 F32 = jnp.float32
 
 SPAN = EL * CAP
-ORDER = (2, 1, 3, 0, 4)
 FAR_FIRST = (2, 6, 3, 5, 4, 1, 7)
 LAG = 8
-SKIP_GROUP = 1
+SKIP_STEP = 1
 OWN = REACH * EL
 
 SEGMENTS = (
@@ -310,9 +309,16 @@
 
     wk_in.wait()
 
-    def project(group):
+    starts = (place_z == 0) & (az >= AZ // 2)
+    flip = starts & (core == 0)
+    order = [REACH]
+    for flag, one, two in ((flip, 1, 3), (flip, 3, 1), (starts, 0, 4), (starts, 4, 0)):
+        order.append(jnp.where(flag, one, two))
+
+    def project(step):
+        group = order[step]
         for place in range(EL):
-            if group * EL + place != OWN:
+            if (step, place) != (0, 0):
                 token_copy(group, (EL - place) % EL).wait_recv()
         rows = recv[pl.ds(group * EL, EL)].reshape(SPAN, D)
         kbuf[group] = nn(rows, wk[...]).astype(BF16)
@@ -325,7 +331,8 @@
     pending = []
     begun = [0]
 
-    def begin(group, chunk, h):
+    def begin(step, chunk, h):
+        group = order[step]
         span = pl.ds(chunk * HALF, HALF)
         lanes = pl.ds((h // 4) * 128, 128)
         slot = begun[0] % (LAG + 1)
@@ -334,19 +341,19 @@
         scores[slot] = raw
         top = jnp.max(raw, axis=0, keepdims=True)
         fade = None
-        if group != ORDER[0]:
+        if step > 0:
             old = best[chunk, h][:1, :]
             top = jnp.maximum(old, top)
             fade = jnp.exp2(old - top)
-        if group != ORDER[-1]:
+        if step < OFFSETS - 1:
             best[chunk, h] = jnp.broadcast_to(top, (8, HALF))
-        pending.append((group, chunk, h, slot, top, fade))
+        pending.append((step, chunk, h, slot, top, fade))
 
     def finish():
-        group, chunk, h, slot, top, fade = pending.pop(0)
+        step, chunk, h, slot, top, fade = pending.pop(0)
         weights = jnp.exp2((scores[slot] - top).astype(BF16))
-        summed = nn(vt[group, h], weights)[: HEAD + 8, :]
-        if group != ORDER[0]:
+        summed = nn(vt[order[step], h], weights)[: HEAD + 8, :]
+        if step > 0:
             summed = summed + acc[chunk, h] * fade
         acc[chunk, h] = summed
 
@@ -396,18 +403,20 @@
     def sends_row(row):
         return (el > 0) if row == 0 else (el < EL - 1)
 
-    def join(chunk, parts):
+    def front(chunk):
         for h in range(HEADS):
             share = acc[chunk, h, :HEAD, :] * (1.0 / acc[chunk, h, HEAD : HEAD + 1, :])
-            att[pl.ds(h * HEAD, HEAD), :] = share.astype(BF16)
-        attended = att[...].T
+            att[chunk, pl.ds(h * HEAD, HEAD), :] = share.astype(BF16)
+        span = pl.ds(chunk * HALF, HALF)
+        residual = pts[span, :].astype(F32) + nn(att[chunk].T, wo[...])
+        return residual, (residual * inv_rms(residual)).astype(BF16)
+
+    def join(chunk, parts, begun, meanwhile=None):
+        result = None
         for rows in parts:
             begin_at, size = min(rows) * 128, len(rows) * 128
             span = pl.ds(chunk * HALF + begin_at, size)
-            residual = pts[span, :].astype(F32) + nn(
-                attended[begin_at : begin_at + size, :], wo[...]
-            )
-            normed = (residual * inv_rms(residual)).astype(BF16)
+            residual, normed = (x[begin_at : begin_at + size, :] for x in begun)
             total = residual
             for block in range(FF // D):
                 cols = pl.ds(block * D, D)
@@ -419,8 +428,8 @@
                     start = place - begin_at
                     joined[row, pl.ds(col, width), :] = total[start : start + width, :]
                     cin[1 + row, pl.ds(PAD + col, width), :] = conv_in[start : start + width, :]
-            for _ in range(len(pending) * len(rows) // 2):
-                finish()
+            if meanwhile is not None:
+                result = meanwhile()
             for row in rows:
 
                 @pl.when(sends_row(row))
@@ -431,23 +440,24 @@
         if chunk == 0:
             for copy in side_copies():
                 copy.start()
+        return result
 
     def skip_part(block):
         cols = pl.ds(block * D, D)
         hs[:, cols] = nn(skp[...], ws[:, cols])
 
-    for group in ORDER[:-1]:
-        project(group)
-        if group == SKIP_GROUP:
+    for step in range(OFFSETS - 1):
+        project(step)
+        if step == SKIP_STEP:
             for copy in skp_in:
                 copy.wait()
             ws_in.wait()
         for chunk in range(2):
             for h in range(HEADS):
-                begin(group, chunk, h)
+                begin(step, chunk, h)
                 if len(pending) > LAG:
                     finish()
-                if group == SKIP_GROUP and h % 4 == 3:
+                if step == SKIP_STEP and h % 4 == 3:
                     skip_part(2 * chunk + h // 4)
     while pending:
         finish()
@@ -455,14 +465,20 @@
     wo_in.wait()
     wh_in.wait()
     wd_in.wait()
-    project(ORDER[-1])
+    project(OFFSETS - 1)
     for chunk in range(2):
         for h in range(HEADS):
-            begin(ORDER[-1], chunk, h)
+            begin(OFFSETS - 1, chunk, h)
             if chunk == 1:
                 finish()
-    join(0, ((1, 0),))
-    join(1, ((1, 0),))
+
+    def second():
+        while pending:
+            finish()
+        return front(1)
+
+    begun_second = join(0, ((1, 0),), front(0), second)
+    join(1, ((1, 0),), begun_second)
 
     for copy in side_copies():
         copy.wait_recv()
@@ -490,23 +506,24 @@
                 for copy in row_copies(chunk, row):
                     copy.wait_send()
 
-    @pl.when(el > 0)
-    def _():
-        for chunk in range(2):
-            for copy in row_copies(chunk, 1):
-                copy.wait_recv()
-
-    upper = nn(jnp.concatenate(taps(0), axis=1), wc[pl.ds(0, 3)].reshape(3 * D, D))
-    out_ref[0] = (joined[0] + upper).astype(BF16)
-
-    @pl.when(el < EL - 1)
-    def _():
-        for chunk in range(2):
-            for copy in row_copies(chunk, 0):
-                copy.wait_recv()
-
-    lower = nn(jnp.concatenate(taps(3), axis=1), wc[pl.ds(6, 3)].reshape(3 * D, D))
-    out_ref[1] = (joined[1] + lower).astype(BF16)
+    for step in range(2):
+        row = jnp.where(el == EL // 2 - 1, step, 1 - step)
+
+        @pl.when((row == 0) & (el > 0))
+        def _():
+            for chunk in range(2):
+                for copy in row_copies(chunk, 1):
+                    copy.wait_recv()
+
+        @pl.when((row == 1) & (el < EL - 1))
+        def _():
+            for chunk in range(2):
+                for copy in row_copies(chunk, 0):
+                    copy.wait_recv()
+
+        beyond = jnp.concatenate(taps(3 * row), axis=1)
+        matrix = wc[pl.ds(6 * row, 3)].reshape(3 * D, D)
+        out_ref[row] = (joined[row] + nn(beyond, matrix)).astype(BF16)
 
 
 def per_device(*args):
@@ -541,7 +558,7 @@
             pltpu.VMEM((2, HEADS, HEAD + 8, HALF), F32),
             pltpu.VMEM((2, HEADS, 8, HALF), F32),
             pltpu.VMEM((LAG + 1, SPAN, HALF), F32),
-            pltpu.VMEM((D, HALF), BF16),
+            pltpu.VMEM((2, D, HALF), BF16),
             pltpu.VMEM((2, COLS, D), F32),
             pltpu.VMEM((4, COLS + 2 * PAD, D), BF16),
             pltpu.VMEM((D, D), BF16),

time: 26.6 us -> 26.2 us (0.985)
  the two profiles are of different devices: /device:TPU:7 before, /device:TPU:6 now
where the time goes in v7:
time: 26.2 us; the launch traced here: 26.1 us
  Pallas kernels  25.4 us (97%)
  local copies, waits for them, and re-layouts  0.71 us (3%)
    pallas_call x1, Pallas kernels, per_device(): pl.pallas_call(kernel, out_shape=pltpu.VMEM((2, COLS, D), BF16), in_specs...  25.4 us
    unnamed x1, local copies, waits for them, and re-layouts  0.71 us

profile of v7, /device:TPU:6, one launch (start us, length us, event | category | flops | bytes accessed | tf_op | source)
XLA Modules:
  0.0 26.1 jit_solution(504782416673187208)
XLA Ops:
  0.0 25.4 %decoder.1 = bf16[2,256,256]{2,1,0:T(8,128)(2,1)S(1)} custom-call(bf16[2,256,256]{2,1,0:T(8,128)(2,1)} %points_hbm.1, bf16[2,256,256]{2,1,0:T(8,128)(2,1)} %skip_hbm.1, bf16[1,1,128,256]{3,2,1,0:T(8,128)(2,1)} %tokens_hbm.1, s32[1,1,5,8,16]{4,3,2,1,0:T(8,128)} %slots_hbm.1, s32[2,16,256]{2,1,0:T(8,128)} %bitcast.1, bf16[256,256]{1,0:T(8,128)(2,1)} %wq_hbm.1, ...), custom_call_target="tpu_custom_call" | custom-call | tf_op jit(solution)/shard_map/decoder/pallas_call | solution.py:532
  25.4 0.7 %copy.15 = bf16[2,256,256]{2,1,0:T(8,128)(2,1)} copy(bf16[2,256,256]{2,1,0:T(8,128)(2,1)S(1)} %decoder.1) | data formatting | bytes 524288

commit v8 on v7

--- a/solution.py
+++ b/solution.py
@@ -428,7 +428,7 @@
                     start = place - begin_at
                     joined[row, pl.ds(col, width), :] = total[start : start + width, :]
                     cin[1 + row, pl.ds(PAD + col, width), :] = conv_in[start : start + width, :]
-            if meanwhile is not None:
+            if meanwhile is not None and rows == parts[-1]:
                 result = meanwhile()
             for row in rows:
 
@@ -477,7 +477,7 @@
             finish()
         return front(1)
 
-    begun_second = join(0, ((1, 0),), front(0), second)
+    begun_second = join(0, ((1,), (0,)), front(0), second)
     join(1, ((1, 0),), begun_second)
 
     for copy in side_copies():

time: 26.2 us -> 26.1 us (level)
  no operation moved by 1% of the time
where the time goes in v8:
time: 26.1 us; the launch traced here: 25.9 us
  Pallas kernels  25.2 us (97%)
  local copies, waits for them, and re-layouts  0.71 us (3%)
    pallas_call x1, Pallas kernels, per_device(): pl.pallas_call(kernel, out_shape=pltpu.VMEM((2, COLS, D), BF16), in_specs...  25.2 us
    unnamed x1, local copies, waits for them, and re-layouts  0.71 us

profile of v8, /device:TPU:6, one launch (start us, length us, event | category | flops | bytes accessed | tf_op | source)
XLA Modules:
  0.0 25.9 jit_solution(6099869827990824698)
XLA Ops:
  0.0 25.2 %decoder.1 = bf16[2,256,256]{2,1,0:T(8,128)(2,1)S(1)} custom-call(bf16[2,256,256]{2,1,0:T(8,128)(2,1)} %points_hbm.1, bf16[2,256,256]{2,1,0:T(8,128)(2,1)} %skip_hbm.1, bf16[1,1,128,256]{3,2,1,0:T(8,128)(2,1)} %tokens_hbm.1, s32[1,1,5,8,16]{4,3,2,1,0:T(8,128)} %slots_hbm.1, s32[2,16,256]{2,1,0:T(8,128)} %bitcast.1, bf16[256,256]{1,0:T(8,128)(2,1)} %wq_hbm.1, ...), custom_call_target="tpu_custom_call" | custom-call | tf_op jit(solution)/shard_map/decoder/pallas_call | solution.py:532
  25.2 0.7 %copy.15 = bf16[2,256,256]{2,1,0:T(8,128)(2,1)} copy(bf16[2,256,256]{2,1,0:T(8,128)(2,1)S(1)} %decoder.1) | data formatting | bytes 524288
